TPU v7x, 32 devices: a whole 2x2x4 slice. The times are simulated.
32 devices in a mesh: gx: 8 (over y, x, core), gz: 4 (over z).
Axes of the slice: x: 2, y: 2, z: 4, core: 2. Of those that a mesh axis runs over, the one named last changes fastest.
Arguments:
- velocity_old: float32 [3, 64, 64, 128], P(None, 'gx', 'gz'), may hold values from -6 to 6
- source: float32 [3, 64, 64, 128], P(None, 'gx', 'gz'), may hold values from -6 to 6
- diag_coef: float32 [64, 64, 128], P('gx', 'gz'), may hold values from 0.5 to 2
- face_coef: float32 [3, 64, 64, 128], P(None, 'gx', 'gz'), may hold values from 0.2 to 2
- bc_flags: int32 [2, 64, 64], P(None, 'gx', 'gz'), may hold values from 0 to 1
- coarse_map: int32 [64, 64, 128], P('gx', 'gz'), may hold values from 0 to 15
- coarse_inverse: float32 [512, 64], P('gx'), may hold values from -0.1 to 0.3
Outputs:
- velocity: float32 [3, 64, 64, 128], P(None, 'gx', 'gz')
- pressure: float32 [64, 64, 128], P('gx', 'gz')
All inputs are finite; a program needn't handle non-finite values.
Results may differ from a plain program's by a relative error of at most 0.0003.
Values sent between devices are 32-bit elements; how exact they have to be, the bound alone decides.
A program may use at most 64 MiB of HBM per device.

v0:
```python
import jax
import jax.numpy as jnp
from jax import lax
from jax.sharding import PartitionSpec as P

COARSE = 16


jacobi_weight = 2.0 / 3.0


def passed_along(value, axis, steps):
    count = lax.axis_size(axis)
    pairs = [(source, (source + steps) % count) for source in range(count)]
    return lax.ppermute(value, axis, pairs)


def with_halo(array, sides, width):
    for axis, dim in sides:
        count, length = (lax.axis_size(axis), array.shape[dim])
        up = [(i, (i + 1) % count) for i in range(count)]
        down = [(j, i) for i, j in up]
        last = lax.slice_in_dim(array, length - width, length, axis=dim)
        initial = lax.slice_in_dim(array, 0, width, axis=dim)
        before = lax.ppermute(last, axis, up)
        after = lax.ppermute(initial, axis, down)
        array = jnp.concatenate([before, array, after], axis=dim)
    return array


def inner_local(left, right):
    return jnp.sum(left * right, axis=(1, 2, 3))


def widen(value):
    return value[:, None, None, None]


def global_sums(pairs):
    local = jnp.stack([inner_local(left, right) for left, right in pairs])
    return lax.psum(local, ("gx", "gz"))


def solve_values(velocity_old, source, diag_coef, face_coef):
    coef_x, coef_z, coef_y = (face_coef[0], face_coef[1], face_coef[2])
    count_y = coef_y.shape[-1]
    level = lax.broadcasted_iota(jnp.int32, coef_y.shape, 2)
    wall = jnp.where((level == 0) | (level == count_y - 1), coef_y[..., -1:], 0.0)
    west_cx = passed_along(coef_x[-1:], "gx", 1)
    south_cz = passed_along(coef_z[:, -1:], "gz", 1)
    wide_cx = jnp.concatenate([west_cx, coef_x], 0)
    wide_cz = jnp.concatenate([south_cz, coef_z], 1)

    def apply(field):
        padded = with_halo(field, (("gx", 1), ("gz", 2)), 1)
        flux_x = wide_cx * (padded[:, :-1, 1:-1] - padded[:, 1:, 1:-1])
        flux_z = wide_cz * (padded[:, 1:-1, :-1] - padded[:, 1:-1, 1:])
        planar = flux_x[:, 1:] - flux_x[:, :-1] + (flux_z[:, :, 1:] - flux_z[:, :, :-1])
        grad_y = coef_y[..., :-1] * (field[..., :-1] - field[..., 1:])
        zero = jnp.zeros_like(field[..., :1])
        vertical = (
            jnp.concatenate([grad_y, zero], -1) - jnp.concatenate([zero, grad_y], -1) + wall * field
        )
        return diag_coef * field + planar + vertical

    x = velocity_old
    r = source - apply(x)
    r0 = r
    p = r
    v = apply(p)
    first = global_sums([(r0, r0), (r0, v)])
    rho = first[0]
    alpha = rho / first[1]
    s = r - widen(alpha) * v
    t = apply(s)
    second = global_sums([(t, s), (t, t), (r0, s), (r0, t)])
    omega = second[0] / second[1]
    x = x + widen(alpha) * p + widen(omega) * s
    r = s - widen(omega) * t
    rho_new = second[2] - omega * second[3]
    beta = rho_new / rho * (alpha / omega)
    p = r + widen(beta) * (p - widen(omega) * v)
    v = apply(p)
    third = global_sums([(r0, v)])
    alpha = rho_new / third[0]
    s = r - widen(alpha) * v
    t = apply(s)
    fourth = global_sums([(t, s), (t, t)])
    omega = fourth[0] / fourth[1]
    return x + widen(alpha) * p + widen(omega) * s


def body(velocity_old, source, diag_coef, face_coef, bc_flags, coarse_map, coarse_inverse):
    coef_y = face_coef[2]
    count_y = coef_y.shape[-1]
    level = lax.broadcasted_iota(jnp.int32, coef_y.shape, 2)
    velocity = solve_values(velocity_old, source, diag_coef, face_coef)
    along_x, along_z, along_y = (velocity[0], velocity[1], velocity[2])
    west_u = passed_along(along_x[-1:], "gx", 1)
    south_w = passed_along(along_z[:, -1:], "gz", 1)
    zero = jnp.zeros_like(along_y[..., :1])
    div = (
        along_x
        - jnp.concatenate([west_u, along_x[:-1]], 0)
        + (along_z - jnp.concatenate([south_w, along_z[:, :-1]], 1))
    )
    div = div + (along_y - jnp.concatenate([zero, along_y[..., :-1]], -1))
    flags = bc_flags.astype(jnp.float32)
    bottom = level == 0
    top = level == count_y - 1
    pdiag = 6.0 - bottom.astype(jnp.float32) - top.astype(jnp.float32)
    pdiag = (
        pdiag
        + jnp.where(bottom, flags[0][..., None], 0.0)
        + jnp.where(top, flags[1][..., None], 0.0)
    )

    def pressure_apply(field):
        padded = with_halo(field, (("gx", 0), ("gz", 1)), 1)
        beside = padded[2:, 1:-1] + padded[:-2, 1:-1] + (padded[1:-1, 2:] + padded[1:-1, :-2])
        beside = beside + (
            jnp.concatenate([field[..., 1:], zero], -1)
            + jnp.concatenate([zero, field[..., :-1]], -1)
        )
        return pdiag * field - beside

    q = jacobi_weight * div / pdiag
    q = q + jacobi_weight * (div - pressure_apply(q)) / pdiag
    res = div - pressure_apply(q)
    labels = lax.broadcasted_iota(jnp.int32, (COARSE, 1, 1, 1), 0)
    onehot = (coarse_map[None] == labels).astype(jnp.float32)
    coarse = jnp.einsum("kxzy,xzy->k", onehot, res, precision=lax.Precision.HIGHEST)
    offset = lax.axis_index("gz") * COARSE
    columns = lax.dynamic_slice_in_dim(coarse_inverse, offset, COARSE, 1)
    own = lax.psum_scatter(
        jnp.dot(columns, coarse, precision=lax.Precision.HIGHEST),
        "gz",
        scatter_dimension=0,
        tiled=True,
    )
    q = q + jnp.einsum("kxzy,k->xzy", onehot, own, precision=lax.Precision.HIGHEST)
    for sweep in range(2):
        q = q + jacobi_weight * (div - pressure_apply(q)) / pdiag
    return (velocity, q)


def solution(mesh):
    placed = (
        P(None, "gx", "gz", None),
        P(None, "gx", "gz", None),
        P("gx", "gz", None),
        P(None, "gx", "gz", None),
        P(None, "gx", "gz"),
        P("gx", "gz", None),
        P("gx", None),
    )
    return jax.shard_map(
        body,
        mesh=mesh,
        in_specs=placed,
        out_specs=(P(None, "gx", "gz", None), P("gx", "gz", None)),
        check_vma=False,
    )
```

profile of v0, /device:TPU:0, one launch (start us, length us, event | category | flops | bytes accessed | tf_op | source)
XLA Modules:
  0.0 278.5 jit_solution(2390331848632894776)
XLA Ops:
  1.6 3.1 %collective-permute-start.3 = (f32[8,1,128]{2,1,0:T(1,128)S(1)}, f32[8,1,128]{2,1,0:T(1,128)S(1)}, u32[]{:S(2)}, u32[]{:S(2)}) collective-permute-start(f32[8,1,128]{2,1,0:T(1,128)S(1)} %slice.567), channel_id=1, source_target_pairs={{0,1},{1,2},{2,3},{3,0},{4,5},{5,6},{6,7},{7,4},{8,9},{9,10},{10,1... | collective-permute-start | bytes 12296 | tf_op jit(solution)/shard_map/ppermute | solution.py:15
  4.8 2.6 collective-permute-start.2
  9.5 2.6 collective-permute-done
  13.8 2.2 collective-permute-start.5
  18.1 2.6 collective-permute-start.7
  23.9 2.5 collective-permute-start.9
  28.4 39.4 %psum.28 = f32[2,3]{1,0:T(2,128)S(1)} all-reduce(f32[2,3]{1,0:T(2,128)S(1)} %pad_maximum_fusion.85), channel_id=1, replica_groups=mesh['gx'=8,'gz'=4] {'gx','gz'}, use_global_device_ids=true, to_apply=%region_2.3 | all-reduce | flops 6 | bytes 48 | tf_op jit(solution)/shard_map/psum | solution.py:41
  68.0 2.6 collective-permute-start.11
  72.2 1.9 collective-permute-start.12
  74.1 2.0 collective-permute-start.13
  78.3 39.7 %psum.29 = f32[4,3]{1,0:T(4,128)S(1)} all-reduce(f32[4,3]{1,0:T(4,128)S(1)} %pad_maximum_fusion.84), channel_id=1, replica_groups=mesh['gx'=8,'gz'=4] {'gx','gz'}, use_global_device_ids=true, to_apply=%region_7.8 | all-reduce | flops 12 | bytes 96 | tf_op jit(solution)/shard_map/psum | solution.py:41
  118.2 2.6 collective-permute-start.15
  122.4 2.1 collective-permute-start.16
  128.5 40.0 %psum.30 = f32[3]{0:T(128)S(1)} all-reduce(f32[3]{0:T(128)S(1)} %get-tuple-element.12), channel_id=1, replica_groups=mesh['gx'=8,'gz'=4] {'gx','gz'}, use_global_device_ids=true, to_apply=%region_9.10 | all-reduce | flops 3 | bytes 24 | tf_op jit(solution)/shard_map/psum | solution.py:41
  168.7 2.6 collective-permute-start.19
  172.9 1.9 collective-permute-start.20
  174.8 2.0 collective-permute-start.21
  179.0 39.7 %psum.31 = f32[2,3]{1,0:T(2,128)S(1)} all-reduce(f32[2,3]{1,0:T(2,128)S(1)} %pad_maximum_fusion.86), channel_id=1, replica_groups=mesh['gx'=8,'gz'=4] {'gx','gz'}, use_global_device_ids=true, to_apply=%region_12.13 | all-reduce | flops 6 | bytes 48 | tf_op jit(solution)/shard_map/psum | solution.py:41
  218.9 2.1 collective-permute-start.23
  221.0 3.3 %collective-permute-done.23 = f32[8,1,128]{2,1,0:T(1,128)S(1)} collective-permute-done((f32[8,1,128]{2,1,0:T(1,128)S(1)}, f32[8,1,128]{2,1,0:T(1,128)S(1)}, u32[]{:S(2)}, u32[]{:S(2)}) %collective-permute-start.23) | collective-permute-done | bytes 4128 | tf_op jit(solution)/shard_map/ppermute | solution.py:15
  226.6 2.6 collective-permute-done.25
  229.3 1.8 collective-permute-start.26
  232.9 3.5 %collective-permute-done.27 = f32[10,1,128]{2,1,0:T(1,128)S(1)} collective-permute-done((f32[10,1,128]{2,1,0:T(1,128)S(1)}, f32[10,1,128]{2,1,0:T(1,128)S(1)}, u32[]{:S(2)}, u32[]{:S(2)}) %collective-permute-start.27) | collective-permute-done | bytes 5152 | tf_op jit(solution)/shard_map/ppermute | solution.py:25
  240.8 2.0 collective-permute-start.31
  244.4 1.9 collective-permute-done.31
  247.4 8.5 %all-reduce.19 = f32[64]{0:T(128)S(1)} all-reduce(f32[64]{0:T(128)S(1)} %convolution_bitcast_fusion), channel_id=2, replica_groups=mesh['gx'=8,'gz'=4] {'gz'}, use_global_device_ids=true, to_apply=%region_13.14.clone | all-reduce | flops 64 | bytes 512
  257.9 2.7 collective-permute-done.33
  260.6 1.9 collective-permute-start.34
  264.3 3.7 %collective-permute-done.35 = f32[10,1,128]{2,1,0:T(1,128)S(1)} collective-permute-done((f32[10,1,128]{2,1,0:T(1,128)S(1)}, f32[10,1,128]{2,1,0:T(1,128)S(1)}, u32[]{:S(2)}, u32[]{:S(2)}) %collective-permute-start.35) | collective-permute-done | bytes 5152 | tf_op jit(solution)/shard_map/ppermute | solution.py:25
  269.5 2.7 collective-permute-done.37
  272.2 2.0 collective-permute-start.39
  275.8 1.9 collective-permute-done.39
  (155 shorter events, 43.8 us)
Async XLA Ops:
  1.6 7.8 %collective-permute-start.3 = (f32[8,1,128]{2,1,0:T(1,128)S(1)}, f32[8,1,128]{2,1,0:T(1,128)S(1)}, u32[]{:S(2)}, u32[]{:S(2)}) collective-permute-start(f32[8,1,128]{2,1,0:T(1,128)S(1)} %slice.567), channel_id=1, source_target_pairs={{0,1},{1,2},{2,3},{3,0},{4,5},{5,6},{6,7},{7,4},{8,9},{9,10},{10,1... | collective-permute-start | bytes 12296 | tf_op jit(solution)/shard_map/ppermute | solution.py:15
  4.7 7.3 %collective-permute-start.1 = (f32[3,1,16,128]{3,2,1,0:T(8,128)S(1)}, f32[3,1,16,128]{3,2,1,0:T(8,128)S(1)}, u32[]{:S(2)}, u32[]{:S(2)}) collective-permute-start(f32[3,1,16,128]{3,2,1,0:T(8,128)S(1)} %get-tuple-element.42), channel_id=1, source_target_pairs={{0,4},{4,8},{8,12},{12,16},{16,20},{20,24},{24,28},{28,0},{1,5},{5... | collective-permute-start | bytes 73736 | tf_op jit(solution)/shard_map/ppermute | solution.py:25
  4.8 7.4 %collective-permute-start.2 = (f32[3,1,16,128]{3,2,1,0:T(8,128)S(1)}, f32[3,1,16,128]{3,2,1,0:T(8,128)S(1)}, u32[]{:S(2)}, u32[]{:S(2)}) collective-permute-start(f32[3,1,16,128]{3,2,1,0:T(8,128)S(1)} %get-tuple-element.41), channel_id=1, source_target_pairs={{4,0},{8,4},{12,8},{16,12},{20,16},{24,20},{28,24},{0,28},{5,1},{9... | collective-permute-start | bytes 73736 | tf_op jit(solution)/shard_map/ppermute | solution.py:26
  8.1 4.0 %collective-permute-start = (f32[1,16,128]{2,1,0:T(8,128)S(1)}, f32[1,16,128]{2,1,0:T(8,128)S(1)}, u32[]{:S(2)}, u32[]{:S(2)}) collective-permute-start(f32[1,16,128]{2,1,0:T(8,128)S(1)} %slice_bitcast_fusion.7), channel_id=1, source_target_pairs={{0,4},{4,8},{8,12},{12,16},{16,20},{20,24},{24,28},{28,0},{1,5},{5... | collective-permute-start | bytes 24584 | tf_op jit(solution)/shard_map/ppermute | solution.py:15
  12.2 5.6 %collective-permute-start.4 = (f32[3,10,1,128]{3,2,1,0:T(1,128)S(1)}, f32[3,10,1,128]{3,2,1,0:T(1,128)S(1)}, u32[]{:S(2)}, u32[]{:S(2)}) collective-permute-start(f32[3,10,1,128]{3,2,1,0:T(1,128)S(1)} %get-tuple-element.26), channel_id=1, source_target_pairs={{0,1},{1,2},{2,3},{3,0},{4,5},{5,6},{6,7},{7,4},{8,9},{9,10},{10,1... | collective-permute-start | bytes 46088 | tf_op jit(solution)/shard_map/ppermute | solution.py:25
  13.8 4.0 %collective-permute-start.5 = (f32[3,10,1,128]{3,2,1,0:T(1,128)S(1)}, f32[3,10,1,128]{3,2,1,0:T(1,128)S(1)}, u32[]{:S(2)}, u32[]{:S(2)}) collective-permute-start(f32[3,10,1,128]{3,2,1,0:T(1,128)S(1)} %get-tuple-element.27), channel_id=1, source_target_pairs={{1,0},{2,1},{3,2},{0,3},{5,4},{6,5},{7,6},{4,7},{9,8},{10,9},{11,1... | collective-permute-start | bytes 46088 | tf_op jit(solution)/shard_map/ppermute | solution.py:26
  18.0 4.4 %collective-permute-start.6 = (f32[3,1,16,128]{3,2,1,0:T(8,128)S(1)}, f32[3,1,16,128]{3,2,1,0:T(8,128)S(1)}, u32[]{:S(2)}, u32[]{:S(2)}) collective-permute-start(f32[3,1,16,128]{3,2,1,0:T(8,128)S(1)} %get-tuple-element.36), channel_id=1, source_target_pairs={{0,4},{4,8},{8,12},{12,16},{16,20},{20,24},{24,28},{28,0},{1,5},{5... | collective-permute-start | bytes 73736 | tf_op jit(solution)/shard_map/ppermute | solution.py:25
  18.1 4.4 %collective-permute-start.7 = (f32[3,1,16,128]{3,2,1,0:T(8,128)S(1)}, f32[3,1,16,128]{3,2,1,0:T(8,128)S(1)}, u32[]{:S(2)}, u32[]{:S(2)}) collective-permute-start(f32[3,1,16,128]{3,2,1,0:T(8,128)S(1)} %get-tuple-element.37), channel_id=1, source_target_pairs={{4,0},{8,4},{12,8},{16,12},{20,16},{24,20},{28,24},{0,28},{5,1},{9... | collective-permute-start | bytes 73736 | tf_op jit(solution)/shard_map/ppermute | solution.py:26
  22.5 5.6 %collective-permute-start.8 = (f32[3,10,1,128]{3,2,1,0:T(1,128)S(1)}, f32[3,10,1,128]{3,2,1,0:T(1,128)S(1)}, u32[]{:S(2)}, u32[]{:S(2)}) collective-permute-start(f32[3,10,1,128]{3,2,1,0:T(1,128)S(1)} %get-tuple-element.24), channel_id=1, source_target_pairs={{0,1},{1,2},{2,3},{3,0},{4,5},{5,6},{6,7},{7,4},{8,9},{9,10},{10,1... | collective-permute-start | bytes 46088 | tf_op jit(solution)/shard_map/ppermute | solution.py:25
  23.9 4.2 %collective-permute-start.9 = (f32[3,10,1,128]{3,2,1,0:T(1,128)S(1)}, f32[3,10,1,128]{3,2,1,0:T(1,128)S(1)}, u32[]{:S(2)}, u32[]{:S(2)}) collective-permute-start(f32[3,10,1,128]{3,2,1,0:T(1,128)S(1)} %get-tuple-element.25), channel_id=1, source_target_pairs={{1,0},{2,1},{3,2},{0,3},{5,4},{6,5},{7,6},{4,7},{9,8},{10,9},{11,1... | collective-permute-start | bytes 46088 | tf_op jit(solution)/shard_map/ppermute | solution.py:26
  67.9 4.2 %collective-permute-start.10 = (f32[3,1,16,128]{3,2,1,0:T(8,128)S(1)}, f32[3,1,16,128]{3,2,1,0:T(8,128)S(1)}, u32[]{:S(2)}, u32[]{:S(2)}) collective-permute-start(f32[3,1,16,128]{3,2,1,0:T(8,128)S(1)} %get-tuple-element.34), channel_id=1, source_target_pairs={{0,4},{4,8},{8,12},{12,16},{16,20},{20,24},{24,28},{28,0},{1,5},{5... | collective-permute-start | bytes 73736 | tf_op jit(solution)/shard_map/ppermute | solution.py:25
  68.0 4.2 %collective-permute-start.11 = (f32[3,1,16,128]{3,2,1,0:T(8,128)S(1)}, f32[3,1,16,128]{3,2,1,0:T(8,128)S(1)}, u32[]{:S(2)}, u32[]{:S(2)}) collective-permute-start(f32[3,1,16,128]{3,2,1,0:T(8,128)S(1)} %get-tuple-element.35), channel_id=1, source_target_pairs={{4,0},{8,4},{12,8},{16,12},{20,16},{24,20},{28,24},{0,28},{5,1},{9... | collective-permute-start | bytes 73736 | tf_op jit(solution)/shard_map/ppermute | solution.py:26
  72.2 5.6 %collective-permute-start.12 = (f32[3,10,1,128]{3,2,1,0:T(1,128)S(1)}, f32[3,10,1,128]{3,2,1,0:T(1,128)S(1)}, u32[]{:S(2)}, u32[]{:S(2)}) collective-permute-start(f32[3,10,1,128]{3,2,1,0:T(1,128)S(1)} %get-tuple-element.22), channel_id=1, source_target_pairs={{0,1},{1,2},{2,3},{3,0},{4,5},{5,6},{6,7},{7,4},{8,9},{9,10},{10,1... | collective-permute-start | bytes 46088 | tf_op jit(solution)/shard_map/ppermute | solution.py:25
  74.1 3.9 %collective-permute-start.13 = (f32[3,10,1,128]{3,2,1,0:T(1,128)S(1)}, f32[3,10,1,128]{3,2,1,0:T(1,128)S(1)}, u32[]{:S(2)}, u32[]{:S(2)}) collective-permute-start(f32[3,10,1,128]{3,2,1,0:T(1,128)S(1)} %get-tuple-element.23), channel_id=1, source_target_pairs={{1,0},{2,1},{3,2},{0,3},{5,4},{6,5},{7,6},{4,7},{9,8},{10,9},{11,1... | collective-permute-start | bytes 46088 | tf_op jit(solution)/shard_map/ppermute | solution.py:26
  118.1 4.2 %collective-permute-start.14 = (f32[3,1,16,128]{3,2,1,0:T(8,128)S(1)}, f32[3,1,16,128]{3,2,1,0:T(8,128)S(1)}, u32[]{:S(2)}, u32[]{:S(2)}) collective-permute-start(f32[3,1,16,128]{3,2,1,0:T(8,128)S(1)} %get-tuple-element.32), channel_id=1, source_target_pairs={{0,4},{4,8},{8,12},{12,16},{16,20},{20,24},{24,28},{28,0},{1,5},{5... | collective-permute-start | bytes 73736 | tf_op jit(solution)/shard_map/ppermute | solution.py:25
  118.2 4.2 %collective-permute-start.15 = (f32[3,1,16,128]{3,2,1,0:T(8,128)S(1)}, f32[3,1,16,128]{3,2,1,0:T(8,128)S(1)}, u32[]{:S(2)}, u32[]{:S(2)}) collective-permute-start(f32[3,1,16,128]{3,2,1,0:T(8,128)S(1)} %get-tuple-element.33), channel_id=1, source_target_pairs={{4,0},{8,4},{12,8},{16,12},{20,16},{24,20},{28,24},{0,28},{5,1},{9... | collective-permute-start | bytes 73736 | tf_op jit(solution)/shard_map/ppermute | solution.py:26
  122.4 5.6 %collective-permute-start.16 = (f32[3,10,1,128]{3,2,1,0:T(1,128)S(1)}, f32[3,10,1,128]{3,2,1,0:T(1,128)S(1)}, u32[]{:S(2)}, u32[]{:S(2)}) collective-permute-start(f32[3,10,1,128]{3,2,1,0:T(1,128)S(1)} %get-tuple-element.20), channel_id=1, source_target_pairs={{0,1},{1,2},{2,3},{3,0},{4,5},{5,6},{6,7},{7,4},{8,9},{9,10},{10,1... | collective-permute-start | bytes 46088 | tf_op jit(solution)/shard_map/ppermute | solution.py:25
  124.5 3.7 %collective-permute-start.17 = (f32[3,10,1,128]{3,2,1,0:T(1,128)S(1)}, f32[3,10,1,128]{3,2,1,0:T(1,128)S(1)}, u32[]{:S(2)}, u32[]{:S(2)}) collective-permute-start(f32[3,10,1,128]{3,2,1,0:T(1,128)S(1)} %get-tuple-element.21), channel_id=1, source_target_pairs={{1,0},{2,1},{3,2},{0,3},{5,4},{6,5},{7,6},{4,7},{9,8},{10,9},{11,1... | collective-permute-start | bytes 46088 | tf_op jit(solution)/shard_map/ppermute | solution.py:26
  168.6 4.2 %collective-permute-start.18 = (f32[3,1,16,128]{3,2,1,0:T(8,128)S(1)}, f32[3,1,16,128]{3,2,1,0:T(8,128)S(1)}, u32[]{:S(2)}, u32[]{:S(2)}) collective-permute-start(f32[3,1,16,128]{3,2,1,0:T(8,128)S(1)} %get-tuple-element.30), channel_id=1, source_target_pairs={{0,4},{4,8},{8,12},{12,16},{16,20},{20,24},{24,28},{28,0},{1,5},{5... | collective-permute-start | bytes 73736 | tf_op jit(solution)/shard_map/ppermute | solution.py:25
  168.7 4.2 %collective-permute-start.19 = (f32[3,1,16,128]{3,2,1,0:T(8,128)S(1)}, f32[3,1,16,128]{3,2,1,0:T(8,128)S(1)}, u32[]{:S(2)}, u32[]{:S(2)}) collective-permute-start(f32[3,1,16,128]{3,2,1,0:T(8,128)S(1)} %get-tuple-element.31), channel_id=1, source_target_pairs={{4,0},{8,4},{12,8},{16,12},{20,16},{24,20},{28,24},{0,28},{5,1},{9... | collective-permute-start | bytes 73736 | tf_op jit(solution)/shard_map/ppermute | solution.py:26
  172.9 5.6 %collective-permute-start.20 = (f32[3,10,1,128]{3,2,1,0:T(1,128)S(1)}, f32[3,10,1,128]{3,2,1,0:T(1,128)S(1)}, u32[]{:S(2)}, u32[]{:S(2)}) collective-permute-start(f32[3,10,1,128]{3,2,1,0:T(1,128)S(1)} %get-tuple-element.18), channel_id=1, source_target_pairs={{0,1},{1,2},{2,3},{3,0},{4,5},{5,6},{6,7},{7,4},{8,9},{9,10},{10,1... | collective-permute-start | bytes 46088 | tf_op jit(solution)/shard_map/ppermute | solution.py:25
  174.8 3.8 %collective-permute-start.21 = (f32[3,10,1,128]{3,2,1,0:T(1,128)S(1)}, f32[3,10,1,128]{3,2,1,0:T(1,128)S(1)}, u32[]{:S(2)}, u32[]{:S(2)}) collective-permute-start(f32[3,10,1,128]{3,2,1,0:T(1,128)S(1)} %get-tuple-element.19), channel_id=1, source_target_pairs={{1,0},{2,1},{3,2},{0,3},{5,4},{6,5},{7,6},{4,7},{9,8},{10,9},{11,1... | collective-permute-start | bytes 46088 | tf_op jit(solution)/shard_map/ppermute | solution.py:26
  218.9 5.5 %collective-permute-start.23 = (f32[8,1,128]{2,1,0:T(1,128)S(1)}, f32[8,1,128]{2,1,0:T(1,128)S(1)}, u32[]{:S(2)}, u32[]{:S(2)}) collective-permute-start(f32[8,1,128]{2,1,0:T(1,128)S(1)} %slice.610), channel_id=1, source_target_pairs={{0,1},{1,2},{2,3},{3,0},{4,5},{5,6},{6,7},{7,4},{8,9},{9,10},{10,1... | collective-permute-start | bytes 12296 | tf_op jit(solution)/shard_map/ppermute | solution.py:15
  221.0 4.0 %collective-permute-start.22 = (f32[1,16,128]{2,1,0:T(8,128)S(1)}, f32[1,16,128]{2,1,0:T(8,128)S(1)}, u32[]{:S(2)}, u32[]{:S(2)}) collective-permute-start(f32[1,16,128]{2,1,0:T(8,128)S(1)} %slice_bitcast_fusion.6), channel_id=1, source_target_pairs={{0,4},{4,8},{8,12},{12,16},{16,20},{20,24},{24,28},{28,0},{1,5},{5... | collective-permute-start | bytes 24584 | tf_op jit(solution)/shard_map/ppermute | solution.py:15
  225.3 4.0 %collective-permute-start.25 = (f32[1,16,128]{2,1,0:T(8,128)S(1)}, f32[1,16,128]{2,1,0:T(8,128)S(1)}, u32[]{:S(2)}, u32[]{:S(2)}) collective-permute-start(f32[1,16,128]{2,1,0:T(8,128)S(1)} %get-tuple-element.65), channel_id=1, source_target_pairs={{0,4},{4,8},{8,12},{12,16},{16,20},{20,24},{24,28},{28,0},{1,5},{5... | collective-permute-start | bytes 24584 | tf_op jit(solution)/shard_map/ppermute | solution.py:25
  231.1 5.4 %collective-permute-start.27 = (f32[10,1,128]{2,1,0:T(1,128)S(1)}, f32[10,1,128]{2,1,0:T(1,128)S(1)}, u32[]{:S(2)}, u32[]{:S(2)}) collective-permute-start(f32[10,1,128]{2,1,0:T(1,128)S(1)} %get-tuple-element.50), channel_id=1, source_target_pairs={{0,1},{1,2},{2,3},{3,0},{4,5},{5,6},{6,7},{7,4},{8,9},{9,10},{10,1... | collective-permute-start | bytes 15368 | tf_op jit(solution)/shard_map/ppermute | solution.py:25
  236.7 4.0 %collective-permute-start.29 = (f32[1,16,128]{2,1,0:T(8,128)S(1)}, f32[1,16,128]{2,1,0:T(8,128)S(1)}, u32[]{:S(2)}, u32[]{:S(2)}) collective-permute-start(f32[1,16,128]{2,1,0:T(8,128)S(1)} %get-tuple-element.61), channel_id=1, source_target_pairs={{0,4},{4,8},{8,12},{12,16},{16,20},{20,24},{24,28},{28,0},{1,5},{5... | collective-permute-start | bytes 24584 | tf_op jit(solution)/shard_map/ppermute | solution.py:25
  240.8 5.5 %collective-permute-start.31 = (f32[10,1,128]{2,1,0:T(1,128)S(1)}, f32[10,1,128]{2,1,0:T(1,128)S(1)}, u32[]{:S(2)}, u32[]{:S(2)}) collective-permute-start(f32[10,1,128]{2,1,0:T(1,128)S(1)} %get-tuple-element.48), channel_id=1, source_target_pairs={{0,1},{1,2},{2,3},{3,0},{4,5},{5,6},{6,7},{7,4},{8,9},{9,10},{10,1... | collective-permute-start | bytes 15368 | tf_op jit(solution)/shard_map/ppermute | solution.py:25
  256.5 4.0 %collective-permute-start.33 = (f32[1,16,128]{2,1,0:T(8,128)S(1)}, f32[1,16,128]{2,1,0:T(8,128)S(1)}, u32[]{:S(2)}, u32[]{:S(2)}) collective-permute-start(f32[1,16,128]{2,1,0:T(8,128)S(1)} %get-tuple-element.57), channel_id=1, source_target_pairs={{0,4},{4,8},{8,12},{12,16},{16,20},{20,24},{24,28},{28,0},{1,5},{5... | collective-permute-start | bytes 24584 | tf_op jit(solution)/shard_map/ppermute | solution.py:25
  262.5 5.4 %collective-permute-start.35 = (f32[10,1,128]{2,1,0:T(1,128)S(1)}, f32[10,1,128]{2,1,0:T(1,128)S(1)}, u32[]{:S(2)}, u32[]{:S(2)}) collective-permute-start(f32[10,1,128]{2,1,0:T(1,128)S(1)} %get-tuple-element.46), channel_id=1, source_target_pairs={{0,1},{1,2},{2,3},{3,0},{4,5},{5,6},{6,7},{7,4},{8,9},{9,10},{10,1... | collective-permute-start | bytes 15368 | tf_op jit(solution)/shard_map/ppermute | solution.py:25
  268.1 4.0 %collective-permute-start.37 = (f32[1,16,128]{2,1,0:T(8,128)S(1)}, f32[1,16,128]{2,1,0:T(8,128)S(1)}, u32[]{:S(2)}, u32[]{:S(2)}) collective-permute-start(f32[1,16,128]{2,1,0:T(8,128)S(1)} %get-tuple-element.53), channel_id=1, source_target_pairs={{0,4},{4,8},{8,12},{12,16},{16,20},{20,24},{24,28},{28,0},{1,5},{5... | collective-permute-start | bytes 24584 | tf_op jit(solution)/shard_map/ppermute | solution.py:25
  272.2 5.5 %collective-permute-start.39 = (f32[10,1,128]{2,1,0:T(1,128)S(1)}, f32[10,1,128]{2,1,0:T(1,128)S(1)}, u32[]{:S(2)}, u32[]{:S(2)}) collective-permute-start(f32[10,1,128]{2,1,0:T(1,128)S(1)} %get-tuple-element.44), channel_id=1, source_target_pairs={{0,1},{1,2},{2,3},{3,0},{4,5},{5,6},{6,7},{7,4},{8,9},{9,10},{10,1... | collective-permute-start | bytes 15368 | tf_op jit(solution)/shard_map/ppermute | solution.py:25
  (16 other events, 284.3 us)
where the time goes:
time: 279 us; the launch traced here: 278 us
  blocking collectives  167 us (60%)
  waiting for transfers between devices  50.3 us (18%)
  starting transfers between devices  48.6 us (17%)
  local copies, waits for them, and re-layouts  4.57 us (2%)
  other arithmetic  4.35 us (2%)
    psum x4, blocking collectives, global_sums(): return lax.psum(local, ('gx', 'gz'))  159 us
    ppermute x18, waiting for transfers between devices, with_halo(): before = lax.ppermute(last, axis, up)  34.2 us
    ppermute x18, starting transfers between devices, with_halo(): after = lax.ppermute(initial, axis, down)  27.8 us
    ppermute x18, starting transfers between devices, with_halo(): before = lax.ppermute(last, axis, up)  15.6 us
    ppermute x18, waiting for transfers between devices, with_halo(): after = lax.ppermute(initial, axis, down)  9.46 us
    unnamed x1, blocking collectives  8.52 us
    ppermute x4, waiting for transfers between devices, passed_along(): return lax.ppermute(value, axis, pairs)  6.56 us
  transfers between devices with their start and end apart: 40, of which 30 were waited for; matrix products, arithmetic and copies ran while one was open for 1% of the time, Pallas kernels for 0%

commit v1 on v0

v1 whole, which is shorter than its diff:
```python
import functools

import jax
import jax.numpy as jnp
from jax import lax
from jax.experimental import pallas as pl
from jax.experimental.pallas import tpu as pltpu
from jax.sharding import PartitionSpec as P

COARSE = 16
PAD = 8

jacobi_weight = 2.0 / 3.0
MESH = pl.DeviceIdType.MESH


def kernel(
    dims,
    x0_ref, src_ref, diag_ref, face_ref, bc_ref, map_ref, inv_ref,
    vel_ref, out_ref,
    fld, xlo, xhi, zlo, zhi, zsend,
    coef_send, coef_x, coef_z,
    prs, pxlo, pxhi, pzlo, pzhi, pzsend,
    dgn, cxl, czl, cyu, cyl,
    msg_x, got_x, msg_z, got_z, msg_c, got_c,
    send_sem, recv_sem, coef_ssem, coef_rsem,
    sum_sx, sum_rx, sum_sz, sum_rz, coarse_s, coarse_r,
):
    n_gx, n_gz, cx_n, cz_n, ny, lanes = dims
    rows = cx_n * cz_n
    gx = lax.axis_index("gx")
    gz = lax.axis_index("gz")
    east = (lax.rem(gx + 1, n_gx), gz)
    west = (lax.rem(gx + n_gx - 1, n_gx), gz)
    north = (gx, lax.rem(gz + 1, n_gz))
    south = (gx, lax.rem(gz + n_gz - 1, n_gz))
    row_x = [(lax.rem(gx + d, n_gx), gz) for d in range(1, n_gx)]
    row_z = [(gx, lax.rem(gz + d, n_gz)) for d in range(1, n_gz)]
    pending = []

    def send(src, dst, ssem, rsem, to):
        copy = pltpu.make_async_remote_copy(
            src_ref=src, dst_ref=dst, send_sem=ssem, recv_sem=rsem,
            device_id=to, device_id_type=MESH,
        )
        copy.start()
        pending.append(copy)
        return copy

    barrier = pltpu.get_barrier_semaphore()
    for other in row_x + row_z:
        pl.semaphore_signal(barrier, inc=1, device_id=other, device_id_type=MESH)
    pl.semaphore_wait(barrier, len(row_x) + len(row_z))

    last = rows - cz_n

    def exchange(phase, src, zs, lo_x, hi_x, lo_z, hi_z):
        zs[0] = src[:, pl.ds(cz_n - 1, cx_n, stride=cz_n), :]
        zs[1] = src[:, pl.ds(0, cx_n, stride=cz_n), :]
        sems = [(send_sem.at[phase, i], recv_sem.at[phase, i]) for i in range(4)]
        return [
            send(zs.at[0], lo_z, *sems[2], north),
            send(zs.at[1], hi_z, *sems[3], south),
            send(src.at[:, pl.ds(last, cz_n), :], lo_x, *sems[0], east),
            send(src.at[:, pl.ds(0, cz_n), :], hi_x, *sems[1], west),
        ]

    def exchange_field(i, src):
        return exchange(i, src, zsend.at[i], xlo.at[i], xhi.at[i], zlo.at[i], zhi.at[i])

    def exchange_pressure(i):
        return exchange(
            5 + i, prs.at[i], pzsend.at[i], pxlo.at[i], pxhi.at[i], pzlo.at[i], pzhi.at[i]
        )

    def arrive(copies):
        for copy in copies:
            copy.wait_recv()

    level = lax.broadcasted_iota(jnp.int32, (rows, ny), 1)
    depth = lax.rem(lax.broadcasted_iota(jnp.int32, (rows, ny), 0), cz_n)
    bottom = level == 0
    top = level == ny - 1
    front = depth == 0
    back = depth == cz_n - 1

    def spread(edge):
        wide = jnp.broadcast_to(edge[..., None, :], edge.shape[:-1] + (cz_n, ny))
        return wide.reshape(edge.shape[:-2] + (rows, ny))

    def x_prev(f, edge):
        return jnp.concatenate([edge, f[..., : rows - cz_n, :]], -2)

    def x_next(f, edge):
        return jnp.concatenate([f[..., cz_n:, :], edge], -2)

    def z_prev(f, edge):
        return jnp.where(front, spread(edge), pltpu.roll(f, 1, f.ndim - 2))

    def z_next(f, edge):
        return jnp.where(back, spread(edge), pltpu.roll(f, rows - 1, f.ndim - 2))

    def y_prev(f):
        return pltpu.roll(f, 1, f.ndim - 1)

    def y_next(f):
        return pltpu.roll(f, ny - 1, f.ndim - 1)

    halo0 = exchange_field(0, x0_ref)
    coef_send[...] = face_ref[1, pl.ds(cz_n - 1, cx_n, stride=cz_n), :]
    coefs = [
        send(face_ref.at[0, pl.ds(last, cz_n), :], coef_x, coef_ssem.at[0], coef_rsem.at[0], east),
        send(coef_send, coef_z, coef_ssem.at[1], coef_rsem.at[1], north),
    ]
    cy = face_ref[2]
    upper = jnp.where(top, 0.0, cy)
    lower = jnp.where(bottom, 0.0, y_prev(cy))
    wall = jnp.where(bottom | top, jnp.broadcast_to(cy[:, ny - 1 :], (rows, ny)), 0.0)
    cyu[...] = upper
    cyl[...] = lower
    base = diag_ref[...] + (face_ref[0] + face_ref[1]) + (upper + lower) + wall
    eye = lax.broadcasted_iota(jnp.int32, (cz_n, cz_n), 0) == lax.broadcasted_iota(
        jnp.int32, (cz_n, cz_n), 1
    )

    def column(side):
        flags = bc_ref[side].astype(jnp.float32)
        parts = [
            jnp.sum(
                jnp.where(eye, jnp.broadcast_to(flags[i : i + 1], (cz_n, cz_n)), 0.0),
                axis=1, keepdims=True,
            )
            for i in range(cx_n)
        ]
        return jnp.broadcast_to(jnp.concatenate(parts, 0), (rows, ny))

    arrive(coefs)
    west_c = x_prev(face_ref[0], coef_x[...])
    south_c = z_prev(face_ref[1], coef_z[...])
    cxl[...] = west_c
    czl[...] = south_c
    dgn[...] = base + (west_c + south_c)

    def apply(f, i):
        total = dgn[...] * f
        total -= face_ref[0] * x_next(f, xhi[i]) + cxl[...] * x_prev(f, xlo[i])
        total -= face_ref[1] * z_next(f, zhi[i]) + czl[...] * z_prev(f, zlo[i])
        total -= cyu[...] * y_next(f) + cyl[...] * y_prev(f)
        return total

    def dots(pairs):
        sums = [jnp.sum(a * b, axis=1, keepdims=True) for a, b in pairs]
        while len(sums) < PAD:
            sums.append(jnp.zeros_like(sums[0]))
        stack = jnp.concatenate(sums, 1).reshape(3 * PAD, ny)
        total = jnp.sum(stack, axis=1, keepdims=True)
        shape = (3 * PAD, 128)
        pick = lax.broadcasted_iota(jnp.int32, shape, 0) == lax.broadcasted_iota(
            jnp.int32, shape, 1
        )
        return jnp.sum(
            jnp.where(pick, jnp.broadcast_to(total, shape), 0.0), axis=0, keepdims=True
        )

    def scatter(msg, got, ssem, rsem, others):
        return [
            send(msg, got.at[d], ssem.at[d], rsem, to) for d, to in enumerate(others)
        ]

    def gathered(msg, got, rsem):
        pltpu.make_async_copy(got, got, rsem).wait()
        return msg[...] + jnp.sum(got[...], axis=0)

    def unpack(total):
        shape = (3 * PAD, 128)
        pick = lax.broadcasted_iota(jnp.int32, shape, 0) == lax.broadcasted_iota(
            jnp.int32, shape, 1
        )
        col = jnp.sum(
            jnp.where(pick, jnp.broadcast_to(total, shape), 0.0), axis=1, keepdims=True
        )
        wide = jnp.broadcast_to(col, (3 * PAD, ny)).reshape(3, PAD, ny)
        return [wide[:, k : k + 1] for k in range(PAD)]

    def sums_start(i, pairs):
        msg_x[i] = dots(pairs)
        scatter(msg_x.at[i], got_x.at[i], sum_sx.at[i], sum_rx.at[i], row_x)

    def sums_turn(i):
        msg_z[i] = gathered(msg_x.at[i], got_x.at[i], sum_rx.at[i])
        scatter(msg_z.at[i], got_z.at[i], sum_sz.at[i], sum_rz.at[i], row_z)

    def sums_end(i):
        return unpack(gathered(msg_z.at[i], got_z.at[i], sum_rz.at[i]))

    arrive(halo0)
    fld[1] = src_ref[...] - apply(x0_ref[...], 0)
    halo = exchange_field(1, fld.at[1])
    pdiag = 6.0 - jnp.where(bottom | top, 1.0, 0.0)
    pdiag = pdiag + jnp.where(bottom, column(0), 0.0) + jnp.where(top, column(1), 0.0)
    share = jacobi_weight / pdiag
    arrive(halo)
    fld[2] = apply(fld[1], 1)
    halo = exchange_field(2, fld.at[2])
    arrive(halo)
    fld[3] = apply(fld[2], 2)
    halo = exchange_field(3, fld.at[3])
    r, v, u = fld[1], fld[2], fld[3]
    sums_start(0, [(r, r), (r, v), (r, u), (v, v), (v, u), (u, u)])
    arrive(halo)
    fld[4] = apply(fld[3], 3)
    halo = exchange_field(4, fld.at[4])
    sums_turn(0)
    arrive(halo)
    z = apply(fld[4], 4)
    rr, rv, ru, vv, vu, uu = sums_end(0)[:6]
    alpha = rr / rv
    omega = (rv - alpha * (vv + ru) + alpha * alpha * vu) / (
        vv - 2.0 * alpha * vu + alpha * alpha * uu
    )
    rho_new = (rr - alpha * rv) - omega * (rv - alpha * ru)
    beta = (rho_new / rr) * (alpha / omega)

    def first(x, r, v, u, y, a, w, b):
        s = r - a * v
        t = v - a * u
        x1 = x + a * r + w * s
        r1 = s - w * t
        p2 = r1 + b * (r - w * v)
        mr1 = t - w * (u - a * y)
        v2 = mr1 + b * (v - w * u)
        return x1, r1, p2, v2, mr1

    r, v, u, y = fld[1], fld[2], fld[3], fld[4]
    x1, r1, p2, v2, mr1 = first(x0_ref[...], r, v, u, y, alpha, omega, beta)
    mv2 = (u - alpha * y) - omega * (y - alpha * z) + beta * (u - omega * y)
    sums_start(
        1,
        [(r, v2), (r1, mr1), (r1, mv2), (v2, mr1), (v2, mv2), (mr1, mr1), (mr1, mv2), (mv2, mv2)],
    )
    fld[5] = x1
    fld[6] = r1
    fld[7] = p2
    fld[8] = v2

    def edge_of(buf, c):
        return first(
            *[buf[i, c] for i in range(5)], alpha[c], omega[c], beta[c]
        )[:4]

    edge_x = edge_of(xlo, 0)
    edge_z = edge_of(zlo, 1)
    sums_turn(1)
    rv2, k1, k2, k3, k4, k5, k6, k7 = sums_end(1)
    alpha2 = rho_new / rv2
    omega2 = (k1 - alpha2 * (k2 + k3) + alpha2 * alpha2 * k4) / (
        k5 - 2.0 * alpha2 * k6 + alpha2 * alpha2 * k7
    )

    def second(x1, r1, p2, v2, a, w):
        return x1 + a * p2 + w * (r1 - a * v2)

    velocity = second(fld[5], fld[6], fld[7], fld[8], alpha2, omega2)
    vel_ref[...] = velocity
    west_u = second(*edge_x, alpha2[0], omega2[0])
    south_w = second(*edge_z, alpha2[1], omega2[1])
    ux, uz, uy = velocity[0], velocity[1], velocity[2]
    div = (ux - x_prev(ux, west_u)) + (uz - z_prev(uz, south_w))
    div = div + (uy - jnp.where(bottom, 0.0, y_prev(uy)))

    def beside(f, i):
        near = x_next(f, pxhi[i, 0]) + x_prev(f, pxlo[i, 0])
        near += z_next(f, pzhi[i, 0]) + z_prev(f, pzlo[i, 0])
        return near + (
            jnp.where(top, 0.0, y_next(f)) + jnp.where(bottom, 0.0, y_prev(f))
        )

    def residual(f, i):
        return div - (pdiag * f - beside(f, i))

    q = share * div
    prs[0, 0] = q
    arrive(exchange_pressure(0))
    q = q + share * residual(q, 0)
    prs[1, 0] = q
    arrive(exchange_pressure(1))
    res = residual(q, 1)
    cells = map_ref[...]
    parts = [
        jnp.sum(jnp.where(cells == m, res, 0.0), axis=0, keepdims=True) for m in range(COARSE)
    ]
    total = jnp.sum(jnp.concatenate(parts, 0), axis=1, keepdims=True)
    shape = (COARSE, lanes)
    place = lax.broadcasted_iota(jnp.int32, shape, 1) == (
        lax.broadcasted_iota(jnp.int32, shape, 0) + gz * COARSE
    )
    msg_c[...] = jnp.sum(
        jnp.where(place, jnp.broadcast_to(total, shape), 0.0), axis=0, keepdims=True
    )
    scatter(msg_c, got_c, coarse_s, coarse_r, row_z)
    coarse = gathered(msg_c, got_c, coarse_r)
    own = inv_ref[pl.ds(pl.multiple_of(gz * COARSE, COARSE), COARSE), :]
    corr = jnp.sum(own * coarse[:, : own.shape[1]], axis=1, keepdims=True)
    corr = jnp.broadcast_to(corr, (COARSE, ny))
    add = jnp.broadcast_to(corr[0:1], (rows, ny))
    for m in range(1, COARSE):
        add = jnp.where(cells == m, corr[m : m + 1], add)
    q = q + add
    for i in (2, 3):
        prs[i, 0] = q
        arrive(exchange_pressure(i))
        q = q + share * residual(q, i)
    out_ref[...] = q
    for copy in pending:
        copy.wait_send()


def body(n_gx, n_gz, velocity_old, source, diag_coef, face_coef, bc_flags, coarse_map, coarse_inverse):
    cx_n, cz_n, ny = diag_coef.shape
    rows = cx_n * cz_n
    group = coarse_inverse.shape[1]
    lanes = -(-group // 128) * 128
    f32 = jnp.float32
    vmem = pltpu.VMEM
    dma = pltpu.SemaphoreType.DMA
    scratch = [
        vmem((9, 3, rows, ny), f32),
        vmem((5, 3, cz_n, ny), f32),
        vmem((5, 3, cz_n, ny), f32),
        vmem((5, 3, cx_n, ny), f32),
        vmem((5, 3, cx_n, ny), f32),
        vmem((5, 2, 3, cx_n, ny), f32),
        vmem((cx_n, ny), f32),
        vmem((cz_n, ny), f32),
        vmem((cx_n, ny), f32),
        vmem((4, 1, rows, ny), f32),
        vmem((4, 1, cz_n, ny), f32),
        vmem((4, 1, cz_n, ny), f32),
        vmem((4, 1, cx_n, ny), f32),
        vmem((4, 1, cx_n, ny), f32),
        vmem((4, 2, 1, cx_n, ny), f32),
        vmem((rows, ny), f32),
        vmem((rows, ny), f32),
        vmem((rows, ny), f32),
        vmem((rows, ny), f32),
        vmem((rows, ny), f32),
        vmem((2, 1, 128), f32),
        vmem((2, n_gx - 1, 1, 128), f32),
        vmem((2, 1, 128), f32),
        vmem((2, n_gz - 1, 1, 128), f32),
        vmem((1, lanes), f32),
        vmem((n_gz - 1, 1, lanes), f32),
        dma((9, 4)),
        dma((9, 4)),
        dma((2,)),
        dma((2,)),
        dma((2, n_gx - 1)),
        dma((2,)),
        dma((2, n_gz - 1)),
        dma((2,)),
        dma((n_gz - 1,)),
        dma,
    ]
    spec = pl.BlockSpec(memory_space=pltpu.VMEM)
    velocity, pressure = pl.pallas_call(
        functools.partial(kernel, (n_gx, n_gz, cx_n, cz_n, ny, lanes)),
        out_shape=(
            jax.ShapeDtypeStruct((3, rows, ny), f32),
            jax.ShapeDtypeStruct((rows, ny), f32),
        ),
        in_specs=[spec] * 7,
        out_specs=(spec, spec),
        scratch_shapes=scratch,
        compiler_params=pltpu.CompilerParams(
            collective_id=0, has_side_effects=True, vmem_limit_bytes=48 * 1024 * 1024
        ),
        name="corrector",
    )(
        velocity_old.reshape(3, rows, ny),
        source.reshape(3, rows, ny),
        diag_coef.reshape(rows, ny),
        face_coef.reshape(3, rows, ny),
        bc_flags,
        coarse_map.reshape(rows, ny),
        coarse_inverse,
    )
    return velocity.reshape(3, cx_n, cz_n, ny), pressure.reshape(cx_n, cz_n, ny)


def solution(mesh):
    placed = (
        P(None, "gx", "gz", None),
        P(None, "gx", "gz", None),
        P("gx", "gz", None),
        P(None, "gx", "gz", None),
        P(None, "gx", "gz"),
        P("gx", "gz", None),
        P("gx", None),
    )
    return jax.shard_map(
        functools.partial(body, mesh.shape["gx"], mesh.shape["gz"]),
        mesh=mesh,
        in_specs=placed,
        out_specs=(P(None, "gx", "gz", None), P("gx", "gz", None)),
        check_vma=False,
    )
```

time: 279 us -> 59 us (0.21)
  blocking collectives: 167 us -> 0 us
  Pallas kernels: 0 us -> 50.7 us
  waiting for transfers between devices: 50.3 us -> 0 us
  starting transfers between devices: 48.6 us -> 0 us
  other arithmetic: 4.35 us -> 0 us
    psum x4 -> x0, blocking collectives: 159 us -> none  [global_sums(): return lax.psum(local, ('gx', 'gz'))]
    pallas_call x0 -> x1, Pallas kernels: none -> 50.7 us  [body(): pl.pallas_call(functools.partial(kernel, (n_gx, n_gz, cx_n, cz_n, ny, lan...]
    ppermute x40 -> x0, waiting for transfers between devices: 50.3 us -> none  [the longest x18 34.2 us: with_halo(): before = lax.ppermute(last, axis, up)]
    ppermute x40 -> x0, starting transfers between devices: 48.6 us -> none  [the longest x18 27.8 us: with_halo(): after = lax.ppermute(initial, axis, down)]
    unnamed x1 -> x0, blocking collectives: 8.52 us -> none
    unnamed x20 -> x16, local copies, waits for them, and re-layouts: 2.26 us -> 7.21 us
  transfers between devices with their start and end apart: 40 -> 0, of which waited for: 30 -> 0; matrix products, arithmetic and copies ran while one was open for 1% -> 0% of each run, Pallas kernels for 0% -> 0%
where the time goes in v1:
time: 59 us; the launch traced here: 58.6 us
  Pallas kernels  50.7 us (86%)
  local copies, waits for them, and re-layouts  7.21 us (12%)
  between operations  0.66 us (1%)
    pallas_call x1, Pallas kernels, body(): pl.pallas_call(functools.partial(kernel, (n_gx, n_gz, cx_n, cz_n, ny, lan...  50.7 us
    unnamed x16, local copies, waits for them, and re-layouts  7.21 us

profile of v1, /device:TPU:0, one launch (start us, length us, event | category | flops | bytes accessed | tf_op | source)
XLA Modules:
  0.0 58.6 jit_solution(7272158756257722968)
XLA Ops:
  0.6 0.0 copy-start.6
  0.6 0.7 %copy-done.6 = s32[2,8,16]{2,1,0:T(8,128)S(1)} copy-done((s32[2,8,16]{2,1,0:T(8,128)S(1)}, s32[2,8,16]{2,1,0:T(8,128)}, u32[]{:S(2)}) %copy-start.6) | copy-done | bytes 1048
  1.3 0.0 copy-start
  1.3 0.9 %copy-done = f32[3,8,16,128]{3,2,1,0:T(8,128)S(1)} copy-done((f32[3,8,16,128]{3,2,1,0:T(8,128)S(1)}, f32[3,8,16,128]{3,2,1,0:T(8,128)}, u32[]{:S(2)}) %copy-start) | copy-done | bytes 196632
  2.3 0.0 copy-start.1
  2.3 0.9 %copy-done.1 = f32[3,8,16,128]{3,2,1,0:T(8,128)S(1)} copy-done((f32[3,8,16,128]{3,2,1,0:T(8,128)S(1)}, f32[3,8,16,128]{3,2,1,0:T(8,128)}, u32[]{:S(2)}) %copy-start.1) | copy-done | bytes 196632
  3.2 0.0 copy-start.2
  3.2 0.9 %copy-done.2 = f32[3,8,16,128]{3,2,1,0:T(8,128)S(1)} copy-done((f32[3,8,16,128]{3,2,1,0:T(8,128)S(1)}, f32[3,8,16,128]{3,2,1,0:T(8,128)}, u32[]{:S(2)}) %copy-start.2) | copy-done | bytes 196632
  4.1 0.0 copy-start.3
  4.1 0.8 %copy-done.3 = f32[8,16,128]{2,1,0:T(8,128)S(1)} copy-done((f32[8,16,128]{2,1,0:T(8,128)S(1)}, f32[8,16,128]{2,1,0:T(8,128)}, u32[]{:S(2)}) %copy-start.3) | copy-done | bytes 65560
  5.0 0.0 copy-start.4
  5.0 0.8 %copy-done.4 = s32[8,16,128]{2,1,0:T(8,128)S(1)} copy-done((s32[8,16,128]{2,1,0:T(8,128)S(1)}, s32[8,16,128]{2,1,0:T(8,128)}, u32[]{:S(2)}) %copy-start.4) | copy-done | bytes 65560
  5.8 0.0 copy-start.5
  5.8 0.8 %copy-done.5 = f32[64,64]{1,0:T(8,128)S(1)} copy-done((f32[64,64]{1,0:T(8,128)S(1)}, f32[64,64]{1,0:T(8,128)}, u32[]{:S(2)}) %copy-start.5) | copy-done | bytes 16408
  6.6 50.7 %corrector.1 = (f32[3,128,128]{2,1,0:T(8,128)S(1)}, f32[128,128]{1,0:T(8,128)S(1)}) custom-call(f32[3,128,128]{2,1,0:T(8,128)S(1)} %bitcast.8, f32[3,128,128]{2,1,0:T(8,128)S(1)} %bitcast.9, f32[128,128]{1,0:T(8,128)S(1)} %bitcast.11, f32[3,128,128]{2,1,0:T(8,128)S(1)} %bitcast.10, s32[2,8,16]{2,1,0:T(8,128)S(1)} %copy-done.6, s32[128,128]{1,0:T(8,128)S(1)} %bitcast.12, ...), custom_call_target="tpu_custom_call" | custom-call | tf_op jit(solution)/shard_map/corrector/pallas_call | solution.py:365
  57.3 0.7 %copy.11 = f32[3,8,16,128]{3,2,1,0:T(8,128)} copy(f32[3,8,16,128]{3,2,1,0:T(8,128)S(1)} %bitcast.7) | data formatting | bytes 393216
  57.9 0.6 %copy.12 = f32[8,16,128]{2,1,0:T(8,128)} copy(f32[8,16,128]{2,1,0:T(8,128)S(1)} %bitcast.13) | data formatting | bytes 131072
Async XLA Ops:
  0.6 0.7 %copy-start.6 = (s32[2,8,16]{2,1,0:T(8,128)S(1)}, s32[2,8,16]{2,1,0:T(8,128)}, u32[]{:S(2)}) copy-start(s32[2,8,16]{2,1,0:T(8,128)} %bc_ref.1) | copy-start | bytes 3076
  1.3 0.9 %copy-start = (f32[3,8,16,128]{3,2,1,0:T(8,128)S(1)}, f32[3,8,16,128]{3,2,1,0:T(8,128)}, u32[]{:S(2)}) copy-start(f32[3,8,16,128]{3,2,1,0:T(8,128)} %param.7) | copy-start | bytes 589828
  2.3 0.9 %copy-start.1 = (f32[3,8,16,128]{3,2,1,0:T(8,128)S(1)}, f32[3,8,16,128]{3,2,1,0:T(8,128)}, u32[]{:S(2)}) copy-start(f32[3,8,16,128]{3,2,1,0:T(8,128)} %param.8) | copy-start | bytes 589828
  3.2 0.9 %copy-start.2 = (f32[3,8,16,128]{3,2,1,0:T(8,128)S(1)}, f32[3,8,16,128]{3,2,1,0:T(8,128)}, u32[]{:S(2)}) copy-start(f32[3,8,16,128]{3,2,1,0:T(8,128)} %param.10) | copy-start | bytes 589828
  4.1 0.8 %copy-start.3 = (f32[8,16,128]{2,1,0:T(8,128)S(1)}, f32[8,16,128]{2,1,0:T(8,128)}, u32[]{:S(2)}) copy-start(f32[8,16,128]{2,1,0:T(8,128)} %param.9) | copy-start | bytes 196612
  5.0 0.8 %copy-start.4 = (s32[8,16,128]{2,1,0:T(8,128)S(1)}, s32[8,16,128]{2,1,0:T(8,128)}, u32[]{:S(2)}) copy-start(s32[8,16,128]{2,1,0:T(8,128)} %param.12) | copy-start | bytes 196612
  5.8 0.8 %copy-start.5 = (f32[64,64]{1,0:T(8,128)S(1)}, f32[64,64]{1,0:T(8,128)}, u32[]{:S(2)}) copy-start(f32[64,64]{1,0:T(8,128)} %inv_ref.1) | copy-start | bytes 49156

commit v2 on v1

--- a/solution.py
+++ b/solution.py
@@ -16,15 +16,20 @@
 
 def kernel(
     dims,
+    x0_in, src_in, diag_in, face_in, bc_in, map_in, inv_in,
+    vel_ref, out_ref,
     x0_ref, src_ref, diag_ref, face_ref, bc_ref, map_ref, inv_ref,
-    vel_ref, out_ref,
     fld, xlo, xhi, zlo, zhi, zsend,
     coef_send, coef_x, coef_z,
     prs, pxlo, pxhi, pzlo, pzhi, pzsend,
+    qxlo, qxhi, qzlo, qzhi, qzsend, qc_send, qc,
+    mxlo, mxhi, mzlo, mzhi, mzsend, mc_send, mc,
+    dxlo, dxhi, dzlo, dzhi, dzsend, inv_w, inv_e,
     dgn, cxl, czl, cyu, cyl,
-    msg_x, got_x, msg_z, got_z, msg_c, got_c,
+    msg_x, got_x, msg_z, got_z, msg_c, got_c, got_w, got_e,
     send_sem, recv_sem, coef_ssem, coef_rsem,
     sum_sx, sum_rx, sum_sz, sum_rz, coarse_s, coarse_r,
+    load_sem, side_s, side_r,
 ):
     n_gx, n_gz, cx_n, cz_n, ny, lanes = dims
     rows = cx_n * cz_n
@@ -47,10 +52,29 @@
         pending.append(copy)
         return copy
 
+    aside_w = [(west[0], to[1]) for to in row_z]
+    aside_e = [(east[0], to[1]) for to in row_z]
+    corners = [
+        (east[0], north[1]), (east[0], south[1]), (west[0], north[1]), (west[0], south[1])
+    ]
+    loads = [
+        pltpu.make_async_copy(a, b, load_sem.at[i])
+        for i, (a, b) in enumerate(
+            [
+                (x0_in, x0_ref), (face_in, face_ref), (diag_in, diag_ref), (src_in, src_ref),
+                (bc_in, bc_ref), (map_in, map_ref), (inv_in, inv_ref),
+            ]
+        )
+    ]
+    for load in loads:
+        load.start()
     barrier = pltpu.get_barrier_semaphore()
-    for other in row_x + row_z:
+    partners = row_x + row_z + aside_w + aside_e
+    for other in partners:
         pl.semaphore_signal(barrier, inc=1, device_id=other, device_id_type=MESH)
-    pl.semaphore_wait(barrier, len(row_x) + len(row_z))
+    loads[0].wait()
+    loads[1].wait()
+    pl.semaphore_wait(barrier, len(partners))
 
     last = rows - cz_n
 
@@ -73,6 +97,22 @@
             5 + i, prs.at[i], pzsend.at[i], pxlo.at[i], pxhi.at[i], pzlo.at[i], pzhi.at[i]
         )
 
+    def exchange_wide(base, f, zs, cs, lo_x, hi_x, lo_z, hi_z, hold):
+        sem = [(side_s.at[base + i], side_r.at[base + i]) for i in range(8)]
+        for k, r in enumerate((rows - 1, last, cz_n - 1, 0)):
+            cs[k] = f[pl.ds(r, 1), :]
+        for k in range(2):
+            zs[0, k] = f[pl.ds(cz_n - 2 + k, cx_n, stride=cz_n), :]
+            zs[1, k] = f[pl.ds(k, cx_n, stride=cz_n), :]
+        copies = [
+            send(cs.at[k], hold.at[k], *sem[k], to) for k, to in enumerate(corners)
+        ]
+        copies.append(send(zs.at[0], lo_z, *sem[4], north))
+        copies.append(send(zs.at[1], hi_z, *sem[5], south))
+        copies.append(send(f.at[pl.ds(last - cz_n, 2 * cz_n), :], lo_x, *sem[6], east))
+        copies.append(send(f.at[pl.ds(0, 2 * cz_n), :], hi_x, *sem[7], west))
+        return copies
+
     def arrive(copies):
         for copy in copies:
             copy.wait_recv()
@@ -118,6 +158,7 @@
     wall = jnp.where(bottom | top, jnp.broadcast_to(cy[:, ny - 1 :], (rows, ny)), 0.0)
     cyu[...] = upper
     cyl[...] = lower
+    loads[2].wait()
     base = diag_ref[...] + (face_ref[0] + face_ref[1]) + (upper + lower) + wall
     eye = lax.broadcasted_iota(jnp.int32, (cz_n, cz_n), 0) == lax.broadcasted_iota(
         jnp.int32, (cz_n, cz_n), 1
@@ -193,12 +234,23 @@
     def sums_end(i):
         return unpack(gathered(msg_z.at[i], got_z.at[i], sum_rz.at[i]))
 
+    for load in loads[3:]:
+        load.wait()
     arrive(halo0)
     fld[1] = src_ref[...] - apply(x0_ref[...], 0)
     halo = exchange_field(1, fld.at[1])
     pdiag = 6.0 - jnp.where(bottom | top, 1.0, 0.0)
     pdiag = pdiag + jnp.where(bottom, column(0), 0.0) + jnp.where(top, column(1), 0.0)
     share = jacobi_weight / pdiag
+    prs[4, 0] = pdiag
+    aside = exchange_wide(
+        0, map_ref, mzsend, mc_send, mxlo, mxhi, mzlo, mzhi, mc
+    )
+    aside.append(send(inv_ref, inv_w, side_s.at[16], side_r.at[16], east))
+    aside.append(send(inv_ref, inv_e, side_s.at[17], side_r.at[17], west))
+    aside += exchange(
+        8, prs.at[4], dzsend, dxlo, dxhi, dzlo, dzhi
+    )
     arrive(halo)
     fld[2] = apply(fld[1], 1)
     halo = exchange_field(2, fld.at[2])
@@ -268,23 +320,61 @@
     div = (ux - x_prev(ux, west_u)) + (uz - z_prev(uz, south_w))
     div = div + (uy - jnp.where(bottom, 0.0, y_prev(uy)))
 
-    def beside(f, i):
-        near = x_next(f, pxhi[i, 0]) + x_prev(f, pxlo[i, 0])
-        near += z_next(f, pzhi[i, 0]) + z_prev(f, pzlo[i, 0])
-        return near + (
-            jnp.where(top, 0.0, y_next(f)) + jnp.where(bottom, 0.0, y_prev(f))
-        )
-
-    def residual(f, i):
-        return div - (pdiag * f - beside(f, i))
+    edge_rows = (cz_n, cz_n, cx_n, cx_n)
+
+    def operate(f, edges):
+        near = x_next(f, edges[1]) + x_prev(f, edges[0])
+        near += z_next(f, edges[3]) + z_prev(f, edges[2])
+        near += jnp.where(top, 0.0, y_next(f)) + jnp.where(bottom, 0.0, y_prev(f))
+        return pdiag * f - near
+
+    def at_face(k, f, beyond, inside, before, after):
+        n = edge_rows[k]
+        pos = lax.broadcasted_iota(jnp.int32, (n, ny), 0)
+        lane = lax.broadcasted_iota(jnp.int32, (n, ny), 1)
+        near = (beyond + inside) + (
+            jnp.where(pos == 0, before, pltpu.roll(f, 1, 0))
+            + jnp.where(pos == n - 1, after, pltpu.roll(f, n - 1, 0))
+        )
+        near += jnp.where(lane == ny - 1, 0.0, y_next(f)) + jnp.where(lane == 0, 0.0, y_prev(f))
+        return face_d[k] * f - near
+
+    def insides(ref):
+        return (
+            ref[pl.ds(0, cz_n), :],
+            ref[pl.ds(last, cz_n), :],
+            ref[pl.ds(0, cx_n, stride=cz_n), :],
+            ref[pl.ds(cz_n - 1, cx_n, stride=cz_n), :],
+        )
+
+    around = ((0, 1), (2, 3), (0, 2), (1, 3))
+
+    def operate_faces(ref, near, far, corner):
+        return [
+            at_face(k, near[k], far[k], inside, corner[around[k][0]], corner[around[k][1]])
+            for k, inside in enumerate(insides(ref))
+        ]
+
+    def split(lo_x, hi_x, lo_z, hi_z):
+        near = (lo_x[cz_n:], hi_x[:cz_n], lo_z[1], hi_z[0])
+        far = (lo_x[:cz_n], hi_x[cz_n:], lo_z[0], hi_z[1])
+        return near, far
 
     q = share * div
-    prs[0, 0] = q
-    arrive(exchange_pressure(0))
-    q = q + share * residual(q, 0)
-    prs[1, 0] = q
-    arrive(exchange_pressure(1))
-    res = residual(q, 1)
+    qref = prs.at[0, 0]
+    qref[...] = q
+    wide = exchange_wide(8, qref, qzsend, qc_send, qxlo, qxhi, qzlo, qzhi, qc)
+    arrive(aside)
+    face_d = (dxlo[0], dxhi[0], dzlo[0], dzhi[0])
+    face_share = [jacobi_weight / d for d in face_d]
+    arrive(wide)
+    near, far = split(qxlo[...], qxhi[...], qzlo[...], qzhi[...])
+    edges = [
+        2.0 * near[k] - face_share[k] * out
+        for k, out in enumerate(operate_faces(qref, near, far, [qc[k] for k in range(4)]))
+    ]
+    q = 2.0 * q - share * operate(q, near)
+    res = div - operate(q, edges)
     cells = map_ref[...]
     parts = [
         jnp.sum(jnp.where(cells == m, res, 0.0), axis=0, keepdims=True) for m in range(COARSE)
@@ -297,20 +387,58 @@
     msg_c[...] = jnp.sum(
         jnp.where(place, jnp.broadcast_to(total, shape), 0.0), axis=0, keepdims=True
     )
-    scatter(msg_c, got_c, coarse_s, coarse_r, row_z)
-    coarse = gathered(msg_c, got_c, coarse_r)
-    own = inv_ref[pl.ds(pl.multiple_of(gz * COARSE, COARSE), COARSE), :]
-    corr = jnp.sum(own * coarse[:, : own.shape[1]], axis=1, keepdims=True)
-    corr = jnp.broadcast_to(corr, (COARSE, ny))
-    add = jnp.broadcast_to(corr[0:1], (rows, ny))
-    for m in range(1, COARSE):
-        add = jnp.where(cells == m, corr[m : m + 1], add)
-    q = q + add
-    for i in (2, 3):
-        prs[i, 0] = q
-        arrive(exchange_pressure(i))
-        q = q + share * residual(q, i)
-    out_ref[...] = q
+    side = n_gz - 1
+    scatter(msg_c, got_w, coarse_s.at[pl.ds(0, n_gz)], coarse_r.at[0], [east] + aside_e)
+    scatter(msg_c, got_e, coarse_s.at[pl.ds(n_gz, n_gz)], coarse_r.at[1], [west] + aside_w)
+    scatter(msg_c, got_c, coarse_s.at[pl.ds(2 * n_gz, side)], coarse_r.at[2], row_z)
+    q = q + share * res
+    prs[1, 0] = q
+    halo = exchange_pressure(1)
+    arrive(halo)
+    q = q + share * (div - operate(q, (pxlo[1, 0], pxhi[1, 0], pzlo[1, 0], pzhi[1, 0])))
+
+    spots = (south[1], gz, north[1])
+
+    def corrections(inv, coarse):
+        out = []
+        for spot in spots:
+            block = inv[pl.ds(pl.multiple_of(spot * COARSE, COARSE), COARSE), :]
+            col = jnp.sum(block * coarse[:, : block.shape[1]], axis=1, keepdims=True)
+            out.append(jnp.broadcast_to(col, (COARSE, ny)))
+        return out
+
+    def lift(cell, corr):
+        add = jnp.broadcast_to(corr[0:1], cell.shape)
+        for m in range(1, COARSE):
+            add = jnp.where(cell == m, corr[m : m + 1], add)
+        return add
+
+    def whole(got, rsem):
+        pltpu.make_async_copy(got, got, rsem).wait()
+        return jnp.sum(got[...], axis=0)
+
+    south_k, own_k, north_k = corrections(inv_ref, gathered(msg_c, got_c, coarse_r.at[2]))
+    west_k = corrections(inv_w, whole(got_w, coarse_r.at[0]))
+    east_k = corrections(inv_e, whole(got_e, coarse_r.at[1]))
+    e = lift(cells, own_k)
+    eref = prs.at[2, 0]
+    eref[...] = e
+    near, far = split(
+        lift(mxlo[...], west_k[1]),
+        lift(mxhi[...], east_k[1]),
+        lift(mzlo[...], south_k),
+        lift(mzhi[...], north_k),
+    )
+    points = [
+        lift(mc[k], c) for k, c in enumerate((west_k[0], west_k[2], east_k[0], east_k[2]))
+    ]
+    edges = [
+        near[k] - face_share[k] * out
+        for k, out in enumerate(operate_faces(eref, near, far, points))
+    ]
+    e = e - share * operate(e, near)
+    e = e - share * operate(e, edges)
+    out_ref[...] = q + e
     for copy in pending:
         copy.wait_send()
 
@@ -323,7 +451,26 @@
     f32 = jnp.float32
     vmem = pltpu.VMEM
     dma = pltpu.SemaphoreType.DMA
+
+    def wide_set(kind):
+        return [
+            vmem((2 * cz_n, ny), kind),
+            vmem((2 * cz_n, ny), kind),
+            vmem((2, cx_n, ny), kind),
+            vmem((2, cx_n, ny), kind),
+            vmem((2, 2, cx_n, ny), kind),
+            vmem((4, 1, ny), kind),
+            vmem((4, 1, ny), kind),
+        ]
+
     scratch = [
+        vmem((3, rows, ny), f32),
+        vmem((3, rows, ny), f32),
+        vmem((rows, ny), f32),
+        vmem((3, rows, ny), f32),
+        vmem(bc_flags.shape, jnp.int32),
+        vmem((rows, ny), jnp.int32),
+        vmem(coarse_inverse.shape, f32),
         vmem((9, 3, rows, ny), f32),
         vmem((5, 3, cz_n, ny), f32),
         vmem((5, 3, cz_n, ny), f32),
@@ -333,12 +480,21 @@
         vmem((cx_n, ny), f32),
         vmem((cz_n, ny), f32),
         vmem((cx_n, ny), f32),
-        vmem((4, 1, rows, ny), f32),
-        vmem((4, 1, cz_n, ny), f32),
-        vmem((4, 1, cz_n, ny), f32),
-        vmem((4, 1, cx_n, ny), f32),
-        vmem((4, 1, cx_n, ny), f32),
-        vmem((4, 2, 1, cx_n, ny), f32),
+        vmem((5, 1, rows, ny), f32),
+        vmem((2, 1, cz_n, ny), f32),
+        vmem((2, 1, cz_n, ny), f32),
+        vmem((2, 1, cx_n, ny), f32),
+        vmem((2, 1, cx_n, ny), f32),
+        vmem((2, 2, 1, cx_n, ny), f32),
+        *wide_set(f32),
+        *wide_set(jnp.int32),
+        vmem((1, cz_n, ny), f32),
+        vmem((1, cz_n, ny), f32),
+        vmem((1, cx_n, ny), f32),
+        vmem((1, cx_n, ny), f32),
+        vmem((2, 1, cx_n, ny), f32),
+        vmem(coarse_inverse.shape, f32),
+        vmem(coarse_inverse.shape, f32),
         vmem((rows, ny), f32),
         vmem((rows, ny), f32),
         vmem((rows, ny), f32),
@@ -350,6 +506,8 @@
         vmem((2, n_gz - 1, 1, 128), f32),
         vmem((1, lanes), f32),
         vmem((n_gz - 1, 1, lanes), f32),
+        vmem((n_gz, 1, lanes), f32),
+        vmem((n_gz, 1, lanes), f32),
         dma((9, 4)),
         dma((9, 4)),
         dma((2,)),
@@ -358,8 +516,11 @@
         dma((2,)),
         dma((2, n_gz - 1)),
         dma((2,)),
-        dma((n_gz - 1,)),
-        dma,
+        dma((3 * n_gz - 1,)),
+        dma((3,)),
+        dma((7,)),
+        dma((18,)),
+        dma((18,)),
     ]
     spec = pl.BlockSpec(memory_space=pltpu.VMEM)
     velocity, pressure = pl.pallas_call(
@@ -368,11 +529,11 @@
             jax.ShapeDtypeStruct((3, rows, ny), f32),
             jax.ShapeDtypeStruct((rows, ny), f32),
         ),
-        in_specs=[spec] * 7,
+        in_specs=[pl.BlockSpec(memory_space=pltpu.HBM)] * 7,
         out_specs=(spec, spec),
         scratch_shapes=scratch,
         compiler_params=pltpu.CompilerParams(
-            collective_id=0, has_side_effects=True, vmem_limit_bytes=48 * 1024 * 1024
+            collective_id=0, has_side_effects=True
         ),
         name="corrector",
     )(

time: 59 us -> 46.6 us (0.79)
  Pallas kernels: 50.7 us -> 43.5 us
  local copies, waits for them, and re-layouts: 7.21 us -> 2.28 us
    pallas_call x1, Pallas kernels: 50.7 us -> 43.5 us  [body(): pl.pallas_call(functools.partial(kernel, (n_gx, n_gz, cx_n, cz_n, ny, lan...]
    unnamed x16 -> x4, local copies, waits for them, and re-layouts: 7.21 us -> 2.28 us
where the time goes in v2:
time: 46.6 us; the launch traced here: 46.4 us
  Pallas kernels  43.5 us (93%)
  local copies, waits for them, and re-layouts  2.28 us (5%)
  between operations  0.65 us (1%)
    pallas_call x1, Pallas kernels, body(): pl.pallas_call(functools.partial(kernel, (n_gx, n_gz, cx_n, cz_n, ny, lan...  43.5 us
    unnamed x4, local copies, waits for them, and re-layouts  2.28 us

profile of v2, /device:TPU:0, one launch (start us, length us, event | category | flops | bytes accessed | tf_op | source)
XLA Modules:
  0.0 46.4 jit_solution(8341226677954550453)
XLA Ops:
  0.6 43.5 %corrector.1 = (f32[3,128,128]{2,1,0:T(8,128)}, f32[128,128]{1,0:T(8,128)}) custom-call(f32[3,128,128]{2,1,0:T(8,128)} %bitcast.8, f32[3,128,128]{2,1,0:T(8,128)} %bitcast.9, f32[128,128]{1,0:T(8,128)} %bitcast.11, f32[3,128,128]{2,1,0:T(8,128)} %bitcast.10, s32[2,8,16]{2,1,0:T(8,128)} %bc_in.1, s32[128,128]{1,0:T(8,128)} %bitcast.12, f32[64,64]{1,0:T(8,128)} %inv_in.1), custom_call_target="tpu_custom_call" | custom-call | tf_op jit(solution)/shard_map/corrector/pallas_call | solution.py:526
  44.1 0.0 copy-start
  44.1 1.6 %copy.11 = f32[3,8,16,128]{3,2,1,0:T(8,128)} copy(f32[3,8,16,128]{3,2,1,0:T(8,128)} %bitcast.7) | data formatting | bytes 393216
  45.8 0.0 copy-done
  45.8 0.6 %copy.12 = f32[8,16,128]{2,1,0:T(8,128)} copy(f32[8,16,128]{2,1,0:T(8,128)S(1)} %bitcast.13) | data formatting | bytes 131072
Async XLA Ops:
  44.1 1.7 %copy-start = (f32[128,128]{1,0:T(8,128)S(1)}, f32[128,128]{1,0:T(8,128)}, u32[]{:S(2)}) copy-start(f32[128,128]{1,0:T(8,128)} %get-tuple-element.5) | copy-start | bytes 196612

commit v3 on v2

--- a/solution.py
+++ b/solution.py
@@ -20,12 +20,13 @@
     vel_ref, out_ref,
     x0_ref, src_ref, diag_ref, face_ref, bc_ref, map_ref, inv_ref,
     fld, xlo, xhi, zlo, zhi, zsend,
+    wxlo, wxhi, wzlo, wzhi, wzsend, wc_send, wc,
     coef_send, coef_x, coef_z,
     prs, pxlo, pxhi, pzlo, pzhi, pzsend,
     qxlo, qxhi, qzlo, qzhi, qzsend, qc_send, qc,
     mxlo, mxhi, mzlo, mzhi, mzsend, mc_send, mc,
     dxlo, dxhi, dzlo, dzhi, dzsend, inv_w, inv_e,
-    dgn, cxl, czl, cyu, cyl,
+    coef, kxlo, kxhi, kzlo, kzhi, kzsend,
     msg_x, got_x, msg_z, got_z, msg_c, got_c, got_w, got_e,
     send_sem, recv_sem, coef_ssem, coef_rsem,
     sum_sx, sum_rx, sum_sz, sum_rz, coarse_s, coarse_r,
@@ -89,28 +90,28 @@
             send(src.at[:, pl.ds(0, cz_n), :], hi_x, *sems[1], west),
         ]
 
-    def exchange_field(i, src):
-        return exchange(i, src, zsend.at[i], xlo.at[i], xhi.at[i], zlo.at[i], zhi.at[i])
-
     def exchange_pressure(i):
         return exchange(
             5 + i, prs.at[i], pzsend.at[i], pxlo.at[i], pxhi.at[i], pzlo.at[i], pzhi.at[i]
         )
 
+    def part(ref, which):
+        return (slice(None),) * (len(ref.shape) - 2) + (which, slice(None))
+
     def exchange_wide(base, f, zs, cs, lo_x, hi_x, lo_z, hi_z, hold):
         sem = [(side_s.at[base + i], side_r.at[base + i]) for i in range(8)]
         for k, r in enumerate((rows - 1, last, cz_n - 1, 0)):
-            cs[k] = f[pl.ds(r, 1), :]
+            cs[k] = f[part(f, pl.ds(r, 1))]
         for k in range(2):
-            zs[0, k] = f[pl.ds(cz_n - 2 + k, cx_n, stride=cz_n), :]
-            zs[1, k] = f[pl.ds(k, cx_n, stride=cz_n), :]
+            zs[0, k] = f[part(f, pl.ds(cz_n - 2 + k, cx_n, stride=cz_n))]
+            zs[1, k] = f[part(f, pl.ds(k, cx_n, stride=cz_n))]
         copies = [
             send(cs.at[k], hold.at[k], *sem[k], to) for k, to in enumerate(corners)
         ]
         copies.append(send(zs.at[0], lo_z, *sem[4], north))
         copies.append(send(zs.at[1], hi_z, *sem[5], south))
-        copies.append(send(f.at[pl.ds(last - cz_n, 2 * cz_n), :], lo_x, *sem[6], east))
-        copies.append(send(f.at[pl.ds(0, 2 * cz_n), :], hi_x, *sem[7], west))
+        copies.append(send(f.at[part(f, pl.ds(last - cz_n, 2 * cz_n))], lo_x, *sem[6], east))
+        copies.append(send(f.at[part(f, pl.ds(0, 2 * cz_n))], hi_x, *sem[7], west))
         return copies
 
     def arrive(copies):
@@ -146,7 +147,7 @@
     def y_next(f):
         return pltpu.roll(f, ny - 1, f.ndim - 1)
 
-    halo0 = exchange_field(0, x0_ref)
+    halo0 = exchange(0, x0_ref, zsend, xlo, xhi, zlo, zhi)
     coef_send[...] = face_ref[1, pl.ds(cz_n - 1, cx_n, stride=cz_n), :]
     coefs = [
         send(face_ref.at[0, pl.ds(last, cz_n), :], coef_x, coef_ssem.at[0], coef_rsem.at[0], east),
@@ -156,8 +157,10 @@
     upper = jnp.where(top, 0.0, cy)
     lower = jnp.where(bottom, 0.0, y_prev(cy))
     wall = jnp.where(bottom | top, jnp.broadcast_to(cy[:, ny - 1 :], (rows, ny)), 0.0)
-    cyu[...] = upper
-    cyl[...] = lower
+    coef[1] = face_ref[0]
+    coef[3] = face_ref[1]
+    coef[5] = upper
+    coef[6] = lower
     loads[2].wait()
     base = diag_ref[...] + (face_ref[0] + face_ref[1]) + (upper + lower) + wall
     eye = lax.broadcasted_iota(jnp.int32, (cz_n, cz_n), 0) == lax.broadcasted_iota(
@@ -178,16 +181,66 @@
     arrive(coefs)
     west_c = x_prev(face_ref[0], coef_x[...])
     south_c = z_prev(face_ref[1], coef_z[...])
-    cxl[...] = west_c
-    czl[...] = south_c
-    dgn[...] = base + (west_c + south_c)
-
-    def apply(f, i):
-        total = dgn[...] * f
-        total -= face_ref[0] * x_next(f, xhi[i]) + cxl[...] * x_prev(f, xlo[i])
-        total -= face_ref[1] * z_next(f, zhi[i]) + czl[...] * z_prev(f, zlo[i])
-        total -= cyu[...] * y_next(f) + cyl[...] * y_prev(f)
+    coef[2] = west_c
+    coef[4] = south_c
+    coef[0] = base + (west_c + south_c)
+
+    def apply(f, edges):
+        total = coef[0] * f
+        total -= coef[1] * x_next(f, edges[1]) + coef[2] * x_prev(f, edges[0])
+        total -= coef[3] * z_next(f, edges[3]) + coef[4] * z_prev(f, edges[2])
+        total -= coef[5] * y_next(f) + coef[6] * y_prev(f)
         return total
+
+    edge_rows = (cz_n, cz_n, cx_n, cx_n)
+    around = ((0, 1), (2, 3), (0, 2), (1, 3))
+
+    def insides(ref):
+        return (
+            ref[part(ref, pl.ds(0, cz_n))],
+            ref[part(ref, pl.ds(last, cz_n))],
+            ref[part(ref, pl.ds(0, cx_n, stride=cz_n))],
+            ref[part(ref, pl.ds(cz_n - 1, cx_n, stride=cz_n))],
+        )
+
+    def split(lo_x, hi_x, lo_z, hi_z):
+        near = (lo_x[..., cz_n:, :], hi_x[..., :cz_n, :], lo_z[1], hi_z[0])
+        far = (lo_x[..., :cz_n, :], hi_x[..., cz_n:, :], lo_z[0], hi_z[1])
+        return near, far
+
+    def along_face(k, f, before, after):
+        n = edge_rows[k]
+        pos = lax.broadcasted_iota(jnp.int32, (n, ny), 0)
+        return (
+            jnp.where(pos == 0, before, pltpu.roll(f, 1, f.ndim - 2)),
+            jnp.where(pos == n - 1, after, pltpu.roll(f, n - 1, f.ndim - 2)),
+        )
+
+    face_coefs = (kxlo, kxhi, kzlo, kzhi)
+
+    def apply_faces(ref, near, far, corner):
+        out = []
+        for k, inside in enumerate(insides(ref)):
+            f, c = near[k], face_coefs[k]
+            down, up = (far[k], inside) if k % 2 == 0 else (inside, far[k])
+            before, after = along_face(k, f, corner[around[k][0]], corner[around[k][1]])
+            n, t = (1, 3) if k < 2 else (3, 1)
+            total = c[0] * f
+            total -= c[n] * up + c[n + 1] * down
+            total -= c[t] * after + c[t + 1] * before
+            total -= c[5] * y_next(f) + c[6] * y_prev(f)
+            out.append(total)
+        return out
+
+    def wide_field(i, ref):
+        return exchange_wide(
+            18 + 8 * i, ref, wzsend.at[i], wc_send.at[i],
+            wxlo.at[i], wxhi.at[i], wzlo.at[i], wzhi.at[i], wc.at[i],
+        )
+
+    def wide_edges(i):
+        near, far = split(wxlo[i], wxhi[i], wzlo[i], wzhi[i])
+        return near, far, [wc[i, k] for k in range(4)]
 
     def dots(pairs):
         sums = [jnp.sum(a * b, axis=1, keepdims=True) for a, b in pairs]
@@ -237,12 +290,23 @@
     for load in loads[3:]:
         load.wait()
     arrive(halo0)
-    fld[1] = src_ref[...] - apply(x0_ref[...], 0)
-    halo = exchange_field(1, fld.at[1])
+    fld[1] = src_ref[...] - apply(x0_ref[...], (xlo[...], xhi[...], zlo[...], zhi[...]))
+    wide = wide_field(0, fld.at[1])
+    aside = exchange(1, coef, kzsend, kxlo, kxhi, kzlo, kzhi)
     pdiag = 6.0 - jnp.where(bottom | top, 1.0, 0.0)
     pdiag = pdiag + jnp.where(bottom, column(0), 0.0) + jnp.where(top, column(1), 0.0)
     share = jacobi_weight / pdiag
     prs[4, 0] = pdiag
+    arrive(wide)
+    r_near, r_far, r_corner = wide_edges(0)
+    v = apply(fld[1], r_near)
+    fld[2] = v
+    arrive(aside)
+    v_near = apply_faces(fld.at[1], r_near, r_far, r_corner)
+    fld[3] = apply(v, v_near)
+    wide = wide_field(1, fld.at[3])
+    r, v, u = fld[1], fld[2], fld[3]
+    sums_start(0, [(r, r), (r, v), (r, u), (v, v), (v, u), (u, u)])
     aside = exchange_wide(
         0, map_ref, mzsend, mc_send, mxlo, mxhi, mzlo, mzhi, mc
     )
@@ -251,20 +315,13 @@
     aside += exchange(
         8, prs.at[4], dzsend, dxlo, dxhi, dzlo, dzhi
     )
-    arrive(halo)
-    fld[2] = apply(fld[1], 1)
-    halo = exchange_field(2, fld.at[2])
-    arrive(halo)
-    fld[3] = apply(fld[2], 2)
-    halo = exchange_field(3, fld.at[3])
-    r, v, u = fld[1], fld[2], fld[3]
-    sums_start(0, [(r, r), (r, v), (r, u), (v, v), (v, u), (u, u)])
-    arrive(halo)
-    fld[4] = apply(fld[3], 3)
-    halo = exchange_field(4, fld.at[4])
     sums_turn(0)
-    arrive(halo)
-    z = apply(fld[4], 4)
+    arrive(wide)
+    u_near, u_far, u_corner = wide_edges(1)
+    y = apply(fld[3], u_near)
+    fld[4] = y
+    y_near = apply_faces(fld.at[3], u_near, u_far, u_corner)
+    z = apply(y, y_near)
     rr, rv, ru, vv, vu, uu = sums_end(0)[:6]
     alpha = rr / rv
     omega = (rv - alpha * (vv + ru) + alpha * alpha * vu) / (
@@ -295,13 +352,15 @@
     fld[7] = p2
     fld[8] = v2
 
-    def edge_of(buf, c):
+    def edge_of(k, c):
+        start = (xlo, xhi, zlo, zhi)[k]
         return first(
-            *[buf[i, c] for i in range(5)], alpha[c], omega[c], beta[c]
+            start[c], r_near[k][c], v_near[k][c], u_near[k][c], y_near[k][c],
+            alpha[c], omega[c], beta[c],
         )[:4]
 
-    edge_x = edge_of(xlo, 0)
-    edge_z = edge_of(zlo, 1)
+    edge_x = edge_of(0, 0)
+    edge_z = edge_of(2, 1)
     sums_turn(1)
     rv2, k1, k2, k3, k4, k5, k6, k7 = sums_end(1)
     alpha2 = rho_new / rv2
@@ -320,8 +379,6 @@
     div = (ux - x_prev(ux, west_u)) + (uz - z_prev(uz, south_w))
     div = div + (uy - jnp.where(bottom, 0.0, y_prev(uy)))
 
-    edge_rows = (cz_n, cz_n, cx_n, cx_n)
-
     def operate(f, edges):
         near = x_next(f, edges[1]) + x_prev(f, edges[0])
         near += z_next(f, edges[3]) + z_prev(f, edges[2])
@@ -329,36 +386,17 @@
         return pdiag * f - near
 
     def at_face(k, f, beyond, inside, before, after):
-        n = edge_rows[k]
-        pos = lax.broadcasted_iota(jnp.int32, (n, ny), 0)
-        lane = lax.broadcasted_iota(jnp.int32, (n, ny), 1)
-        near = (beyond + inside) + (
-            jnp.where(pos == 0, before, pltpu.roll(f, 1, 0))
-            + jnp.where(pos == n - 1, after, pltpu.roll(f, n - 1, 0))
-        )
+        lane = lax.broadcasted_iota(jnp.int32, f.shape, 1)
+        before, after = along_face(k, f, before, after)
+        near = (beyond + inside) + (before + after)
         near += jnp.where(lane == ny - 1, 0.0, y_next(f)) + jnp.where(lane == 0, 0.0, y_prev(f))
         return face_d[k] * f - near
-
-    def insides(ref):
-        return (
-            ref[pl.ds(0, cz_n), :],
-            ref[pl.ds(last, cz_n), :],
-            ref[pl.ds(0, cx_n, stride=cz_n), :],
-            ref[pl.ds(cz_n - 1, cx_n, stride=cz_n), :],
-        )
-
-    around = ((0, 1), (2, 3), (0, 2), (1, 3))
 
     def operate_faces(ref, near, far, corner):
         return [
             at_face(k, near[k], far[k], inside, corner[around[k][0]], corner[around[k][1]])
             for k, inside in enumerate(insides(ref))
         ]
-
-    def split(lo_x, hi_x, lo_z, hi_z):
-        near = (lo_x[cz_n:], hi_x[:cz_n], lo_z[1], hi_z[0])
-        far = (lo_x[:cz_n], hi_x[cz_n:], lo_z[0], hi_z[1])
-        return near, far
 
     q = share * div
     qref = prs.at[0, 0]
@@ -472,11 +510,18 @@
         vmem((rows, ny), jnp.int32),
         vmem(coarse_inverse.shape, f32),
         vmem((9, 3, rows, ny), f32),
-        vmem((5, 3, cz_n, ny), f32),
-        vmem((5, 3, cz_n, ny), f32),
-        vmem((5, 3, cx_n, ny), f32),
-        vmem((5, 3, cx_n, ny), f32),
-        vmem((5, 2, 3, cx_n, ny), f32),
+        vmem((3, cz_n, ny), f32),
+        vmem((3, cz_n, ny), f32),
+        vmem((3, cx_n, ny), f32),
+        vmem((3, cx_n, ny), f32),
+        vmem((2, 3, cx_n, ny), f32),
+        vmem((2, 3, 2 * cz_n, ny), f32),
+        vmem((2, 3, 2 * cz_n, ny), f32),
+        vmem((2, 2, 3, cx_n, ny), f32),
+        vmem((2, 2, 3, cx_n, ny), f32),
+        vmem((2, 2, 2, 3, cx_n, ny), f32),
+        vmem((2, 4, 3, 1, ny), f32),
+        vmem((2, 4, 3, 1, ny), f32),
         vmem((cx_n, ny), f32),
         vmem((cz_n, ny), f32),
         vmem((cx_n, ny), f32),
@@ -495,11 +540,12 @@
         vmem((2, 1, cx_n, ny), f32),
         vmem(coarse_inverse.shape, f32),
         vmem(coarse_inverse.shape, f32),
-        vmem((rows, ny), f32),
-        vmem((rows, ny), f32),
-        vmem((rows, ny), f32),
-        vmem((rows, ny), f32),
-        vmem((rows, ny), f32),
+        vmem((7, rows, ny), f32),
+        vmem((7, cz_n, ny), f32),
+        vmem((7, cz_n, ny), f32),
+        vmem((7, cx_n, ny), f32),
+        vmem((7, cx_n, ny), f32),
+        vmem((2, 7, cx_n, ny), f32),
         vmem((2, 1, 128), f32),
         vmem((2, n_gx - 1, 1, 128), f32),
         vmem((2, 1, 128), f32),
@@ -519,8 +565,8 @@
         dma((3 * n_gz - 1,)),
         dma((3,)),
         dma((7,)),
-        dma((18,)),
-        dma((18,)),
+        dma((34,)),
+        dma((34,)),
     ]
     spec = pl.BlockSpec(memory_space=pltpu.VMEM)
     velocity, pressure = pl.pallas_call(
@@ -533,7 +579,7 @@
         out_specs=(spec, spec),
         scratch_shapes=scratch,
         compiler_params=pltpu.CompilerParams(
-            collective_id=0, has_side_effects=True
+            collective_id=0, has_side_effects=True, vmem_limit_bytes=48 * 1024 * 1024
         ),
         name="corrector",
     )(

time: 46.6 us -> 49.1 us (1.054)
  local copies, waits for them, and re-layouts: 2.28 us -> 7.21 us
  Pallas kernels: 43.5 us -> 40.8 us
    unnamed x4 -> x16, local copies, waits for them, and re-layouts: 2.28 us -> 7.21 us
    pallas_call x1, Pallas kernels: 43.5 us -> 40.8 us  [body(): pl.pallas_call(functools.partial(kernel, (n_gx, n_gz, cx_n, cz_n, ny, lan...]
where the time goes in v3:
time: 49.1 us; the launch traced here: 48.7 us
  Pallas kernels  40.8 us (83%)
  local copies, waits for them, and re-layouts  7.21 us (15%)
  between operations  0.66 us (1%)
    pallas_call x1, Pallas kernels, body(): pl.pallas_call(functools.partial(kernel, (n_gx, n_gz, cx_n, cz_n, ny, lan...  40.8 us
    unnamed x16, local copies, waits for them, and re-layouts  7.21 us

profile of v3, /device:TPU:0, one launch (start us, length us, event | category | flops | bytes accessed | tf_op | source)
XLA Modules:
  0.0 48.7 jit_solution(4811078660411305626)
XLA Ops:
  0.6 0.0 copy-start.6
  0.6 0.7 %copy-done.6 = s32[2,8,16]{2,1,0:T(8,128)S(1)} copy-done((s32[2,8,16]{2,1,0:T(8,128)S(1)}, s32[2,8,16]{2,1,0:T(8,128)}, u32[]{:S(2)}) %copy-start.6) | copy-done | bytes 1048
  1.3 0.0 copy-start
  1.3 0.9 %copy-done = f32[3,8,16,128]{3,2,1,0:T(8,128)S(1)} copy-done((f32[3,8,16,128]{3,2,1,0:T(8,128)S(1)}, f32[3,8,16,128]{3,2,1,0:T(8,128)}, u32[]{:S(2)}) %copy-start) | copy-done | bytes 196632
  2.3 0.0 copy-start.1
  2.3 0.9 %copy-done.1 = f32[3,8,16,128]{3,2,1,0:T(8,128)S(1)} copy-done((f32[3,8,16,128]{3,2,1,0:T(8,128)S(1)}, f32[3,8,16,128]{3,2,1,0:T(8,128)}, u32[]{:S(2)}) %copy-start.1) | copy-done | bytes 196632
  3.2 0.0 copy-start.2
  3.2 0.9 %copy-done.2 = f32[3,8,16,128]{3,2,1,0:T(8,128)S(1)} copy-done((f32[3,8,16,128]{3,2,1,0:T(8,128)S(1)}, f32[3,8,16,128]{3,2,1,0:T(8,128)}, u32[]{:S(2)}) %copy-start.2) | copy-done | bytes 196632
  4.1 0.0 copy-start.3
  4.1 0.8 %copy-done.3 = f32[8,16,128]{2,1,0:T(8,128)S(1)} copy-done((f32[8,16,128]{2,1,0:T(8,128)S(1)}, f32[8,16,128]{2,1,0:T(8,128)}, u32[]{:S(2)}) %copy-start.3) | copy-done | bytes 65560
  5.0 0.0 copy-start.4
  5.0 0.8 %copy-done.4 = s32[8,16,128]{2,1,0:T(8,128)S(1)} copy-done((s32[8,16,128]{2,1,0:T(8,128)S(1)}, s32[8,16,128]{2,1,0:T(8,128)}, u32[]{:S(2)}) %copy-start.4) | copy-done | bytes 65560
  5.8 0.0 copy-start.5
  5.8 0.8 %copy-done.5 = f32[64,64]{1,0:T(8,128)S(1)} copy-done((f32[64,64]{1,0:T(8,128)S(1)}, f32[64,64]{1,0:T(8,128)}, u32[]{:S(2)}) %copy-start.5) | copy-done | bytes 16408
  6.6 40.8 %corrector.1 = (f32[3,128,128]{2,1,0:T(8,128)S(1)}, f32[128,128]{1,0:T(8,128)S(1)}) custom-call(f32[3,128,128]{2,1,0:T(8,128)S(1)} %bitcast.8, f32[3,128,128]{2,1,0:T(8,128)S(1)} %bitcast.9, f32[128,128]{1,0:T(8,128)S(1)} %bitcast.11, f32[3,128,128]{2,1,0:T(8,128)S(1)} %bitcast.10, s32[2,8,16]{2,1,0:T(8,128)S(1)} %copy-done.6, s32[128,128]{1,0:T(8,128)S(1)} %bitcast.12, ...), custom_call_target="tpu_custom_call" | custom-call | tf_op jit(solution)/shard_map/corrector/pallas_call | solution.py:572
  47.4 0.7 %copy.11 = f32[3,8,16,128]{3,2,1,0:T(8,128)} copy(f32[3,8,16,128]{3,2,1,0:T(8,128)S(1)} %bitcast.7) | data formatting | bytes 393216
  48.0 0.6 %copy.12 = f32[8,16,128]{2,1,0:T(8,128)} copy(f32[8,16,128]{2,1,0:T(8,128)S(1)} %bitcast.13) | data formatting | bytes 131072
Async XLA Ops:
  0.6 0.7 %copy-start.6 = (s32[2,8,16]{2,1,0:T(8,128)S(1)}, s32[2,8,16]{2,1,0:T(8,128)}, u32[]{:S(2)}) copy-start(s32[2,8,16]{2,1,0:T(8,128)} %bc_in.1) | copy-start | bytes 3076
  1.3 0.9 %copy-start = (f32[3,8,16,128]{3,2,1,0:T(8,128)S(1)}, f32[3,8,16,128]{3,2,1,0:T(8,128)}, u32[]{:S(2)}) copy-start(f32[3,8,16,128]{3,2,1,0:T(8,128)} %param.7) | copy-start | bytes 589828
  2.3 0.9 %copy-start.1 = (f32[3,8,16,128]{3,2,1,0:T(8,128)S(1)}, f32[3,8,16,128]{3,2,1,0:T(8,128)}, u32[]{:S(2)}) copy-start(f32[3,8,16,128]{3,2,1,0:T(8,128)} %param.8) | copy-start | bytes 589828
  3.2 0.9 %copy-start.2 = (f32[3,8,16,128]{3,2,1,0:T(8,128)S(1)}, f32[3,8,16,128]{3,2,1,0:T(8,128)}, u32[]{:S(2)}) copy-start(f32[3,8,16,128]{3,2,1,0:T(8,128)} %param.10) | copy-start | bytes 589828
  4.1 0.8 %copy-start.3 = (f32[8,16,128]{2,1,0:T(8,128)S(1)}, f32[8,16,128]{2,1,0:T(8,128)}, u32[]{:S(2)}) copy-start(f32[8,16,128]{2,1,0:T(8,128)} %param.9) | copy-start | bytes 196612
  5.0 0.8 %copy-start.4 = (s32[8,16,128]{2,1,0:T(8,128)S(1)}, s32[8,16,128]{2,1,0:T(8,128)}, u32[]{:S(2)}) copy-start(s32[8,16,128]{2,1,0:T(8,128)} %param.12) | copy-start | bytes 196612
  5.8 0.8 %copy-start.5 = (f32[64,64]{1,0:T(8,128)S(1)}, f32[64,64]{1,0:T(8,128)}, u32[]{:S(2)}) copy-start(f32[64,64]{1,0:T(8,128)} %inv_in.1) | copy-start | bytes 49156

commit v4 on v3

--- a/solution.py
+++ b/solution.py
@@ -17,7 +17,7 @@
 def kernel(
     dims,
     x0_in, src_in, diag_in, face_in, bc_in, map_in, inv_in,
-    vel_ref, out_ref,
+    vel_a, vel_b, prs_a, prs_b,
     x0_ref, src_ref, diag_ref, face_ref, bc_ref, map_ref, inv_ref,
     fld, xlo, xhi, zlo, zhi, zsend,
     wxlo, wxhi, wzlo, wzhi, wzsend, wc_send, wc,
@@ -30,7 +30,7 @@
     msg_x, got_x, msg_z, got_z, msg_c, got_c, got_w, got_e,
     send_sem, recv_sem, coef_ssem, coef_rsem,
     sum_sx, sum_rx, sum_sz, sum_rz, coarse_s, coarse_r,
-    load_sem, side_s, side_r,
+    load_sem, side_s, side_r, store_sem,
 ):
     n_gx, n_gz, cx_n, cz_n, ny, lanes = dims
     rows = cx_n * cz_n
@@ -369,12 +369,20 @@
     )
 
     def second(x1, r1, p2, v2, a, w):
-        return x1 + a * p2 + w * (r1 - a * v2)
-
-    velocity = second(fld[5], fld[6], fld[7], fld[8], alpha2, omega2)
-    vel_ref[...] = velocity
-    west_u = second(*edge_x, alpha2[0], omega2[0])
-    south_w = second(*edge_z, alpha2[1], omega2[1])
+        return x1 + a * p2, w * (r1 - a * v2)
+
+    def put(i, src, dst):
+        copy = pltpu.make_async_copy(src, dst, store_sem.at[i])
+        copy.start()
+        return copy
+
+    first_half, second_half = second(fld[5], fld[6], fld[7], fld[8], alpha2, omega2)
+    fld[0] = first_half
+    fld[9] = second_half
+    stores = [put(0, fld.at[0], vel_a), put(1, fld.at[9], vel_b)]
+    velocity = first_half + second_half
+    west_u = sum(second(*edge_x, alpha2[0], omega2[0]))
+    south_w = sum(second(*edge_z, alpha2[1], omega2[1]))
     ux, uz, uy = velocity[0], velocity[1], velocity[2]
     div = (ux - x_prev(ux, west_u)) + (uz - z_prev(uz, south_w))
     div = div + (uy - jnp.where(bottom, 0.0, y_prev(uy)))
@@ -434,6 +442,8 @@
     halo = exchange_pressure(1)
     arrive(halo)
     q = q + share * (div - operate(q, (pxlo[1, 0], pxhi[1, 0], pzlo[1, 0], pzhi[1, 0])))
+    prs[3, 0] = q
+    stores.append(put(2, prs.at[3, 0], prs_a))
 
     spots = (south[1], gz, north[1])
 
@@ -476,7 +486,10 @@
     ]
     e = e - share * operate(e, near)
     e = e - share * operate(e, edges)
-    out_ref[...] = q + e
+    prs[5, 0] = e
+    stores.append(put(3, prs.at[5, 0], prs_b))
+    for copy in stores:
+        copy.wait()
     for copy in pending:
         copy.wait_send()
 
@@ -509,7 +522,7 @@
         vmem(bc_flags.shape, jnp.int32),
         vmem((rows, ny), jnp.int32),
         vmem(coarse_inverse.shape, f32),
-        vmem((9, 3, rows, ny), f32),
+        vmem((10, 3, rows, ny), f32),
         vmem((3, cz_n, ny), f32),
         vmem((3, cz_n, ny), f32),
         vmem((3, cx_n, ny), f32),
@@ -525,7 +538,7 @@
         vmem((cx_n, ny), f32),
         vmem((cz_n, ny), f32),
         vmem((cx_n, ny), f32),
-        vmem((5, 1, rows, ny), f32),
+        vmem((6, 1, rows, ny), f32),
         vmem((2, 1, cz_n, ny), f32),
         vmem((2, 1, cz_n, ny), f32),
         vmem((2, 1, cx_n, ny), f32),
@@ -567,19 +580,22 @@
         dma((7,)),
         dma((34,)),
         dma((34,)),
-    ]
-    spec = pl.BlockSpec(memory_space=pltpu.VMEM)
-    velocity, pressure = pl.pallas_call(
+        dma((4,)),
+    ]
+    spec = pl.BlockSpec(memory_space=pltpu.HBM)
+    vel_a, vel_b, prs_a, prs_b = pl.pallas_call(
         functools.partial(kernel, (n_gx, n_gz, cx_n, cz_n, ny, lanes)),
         out_shape=(
             jax.ShapeDtypeStruct((3, rows, ny), f32),
+            jax.ShapeDtypeStruct((3, rows, ny), f32),
+            jax.ShapeDtypeStruct((rows, ny), f32),
             jax.ShapeDtypeStruct((rows, ny), f32),
         ),
-        in_specs=[pl.BlockSpec(memory_space=pltpu.HBM)] * 7,
-        out_specs=(spec, spec),
+        in_specs=[spec] * 7,
+        out_specs=(spec,) * 4,
         scratch_shapes=scratch,
         compiler_params=pltpu.CompilerParams(
-            collective_id=0, has_side_effects=True, vmem_limit_bytes=48 * 1024 * 1024
+            collective_id=0, has_side_effects=True
         ),
         name="corrector",
     )(
@@ -591,7 +607,8 @@
         coarse_map.reshape(rows, ny),
         coarse_inverse,
     )
-    return velocity.reshape(3, cx_n, cz_n, ny), pressure.reshape(cx_n, cz_n, ny)
+    velocity = (vel_a + vel_b).reshape(3, cx_n, cz_n, ny)
+    return velocity, (prs_a + prs_b).reshape(cx_n, cz_n, ny)
 
 
 def solution(mesh):

time: 49.1 us -> 44.6 us (0.908)
  local copies, waits for them, and re-layouts: 7.21 us -> 0.01 us
  other arithmetic: 0 us -> 3.18 us
    unnamed x16 -> x2, local copies, waits for them, and re-layouts: 7.21 us -> 0.01 us
    add x0 -> x2, other arithmetic: none -> 3.18 us  [the longest x1 1.63 us: body(): velocity = (vel_a + vel_b).reshape(3, cx_n, cz_n, ny)]
where the time goes in v4:
time: 44.6 us; the launch traced here: 44.4 us
  Pallas kernels  40.6 us (91%)
  other arithmetic  3.18 us (7%)
  between operations  0.65 us (1%)
    pallas_call x1, Pallas kernels, body(): pl.pallas_call(functools.partial(kernel, (n_gx, n_gz, cx_n, cz_n, ny, lan...  40.6 us
    add x1, other arithmetic, body(): velocity = (vel_a + vel_b).reshape(3, cx_n, cz_n, ny)  1.63 us
    add x1, other arithmetic, body(): return (velocity, (prs_a + prs_b).reshape(cx_n, cz_n, ny))  1.55 us

profile of v4, /device:TPU:0, one launch (start us, length us, event | category | flops | bytes accessed | tf_op | source)
XLA Modules:
  0.0 44.4 jit_solution(15452405813092114382)
XLA Ops:
  0.6 40.6 %corrector.1 = (f32[3,128,128]{2,1,0:T(8,128)}, f32[3,128,128]{2,1,0:T(8,128)}, f32[128,128]{1,0:T(8,128)}, f32[128,128]{1,0:T(8,128)}) custom-call(f32[3,128,128]{2,1,0:T(8,128)} %bitcast.7, f32[3,128,128]{2,1,0:T(8,128)} %bitcast.8, f32[128,128]{1,0:T(8,128)} %bitcast.11, f32[3,128,128]{2,1,0:T(8,128)} %bitcast.9, s32[2,8,16]{2,1,0:T(8,128)} %bc_in.1, ...), custom_call_target="tpu_custom_call" | custom-call | tf_op jit(solution)/shard_map/corrector/pallas_call | solution.py:586
  41.2 0.0 copy-start
  41.2 1.5 %add.7 = f32[128,128]{1,0:T(8,128)} add(f32[128,128]{1,0:T(8,128)} %get-tuple-element.8, f32[128,128]{1,0:T(8,128)} %get-tuple-element.9) | non-fusion elementwise | flops 16384 | bytes 196608 | tf_op jit(solution)/shard_map/add | solution.py:611
  42.7 0.0 copy-done
  42.8 1.6 %add.6 = f32[3,128,128]{2,1,0:T(8,128)} add(f32[3,128,128]{2,1,0:T(8,128)S(1)} %copy-done, f32[3,128,128]{2,1,0:T(8,128)} %get-tuple-element.7) | non-fusion elementwise | flops 49152 | bytes 589824 | tf_op jit(solution)/shard_map/add | solution.py:610
Async XLA Ops:
  41.2 1.6 %copy-start = (f32[3,128,128]{2,1,0:T(8,128)S(1)}, f32[3,128,128]{2,1,0:T(8,128)}, u32[]{:S(2)}) copy-start(f32[3,128,128]{2,1,0:T(8,128)} %get-tuple-element.6) | copy-start | bytes 589828

commit v5 on v3

--- a/solution.py
+++ b/solution.py
@@ -583,13 +583,18 @@
         ),
         name="corrector",
     )(
-        velocity_old.reshape(3, rows, ny),
-        source.reshape(3, rows, ny),
-        diag_coef.reshape(rows, ny),
-        face_coef.reshape(3, rows, ny),
-        bc_flags,
-        coarse_map.reshape(rows, ny),
-        coarse_inverse,
+        *[
+            pltpu.with_memory_space_constraint(a, pltpu.HBM)
+            for a in (
+                velocity_old.reshape(3, rows, ny),
+                source.reshape(3, rows, ny),
+                diag_coef.reshape(rows, ny),
+                face_coef.reshape(3, rows, ny),
+                bc_flags,
+                coarse_map.reshape(rows, ny),
+                coarse_inverse,
+            )
+        ]
     )
     return velocity.reshape(3, cx_n, cz_n, ny), pressure.reshape(cx_n, cz_n, ny)
 

time: 49.1 us -> 42 us (0.86)
  local copies, waits for them, and re-layouts: 7.21 us -> 1.31 us
  Pallas kernels: 40.8 us -> 39.9 us
    unnamed x16 -> x2, local copies, waits for them, and re-layouts: 7.21 us -> 1.31 us
    pallas_call x1, Pallas kernels: 40.8 us -> 39.9 us  [body(): pl.pallas_call(functools.partial(kernel, (n_gx, n_gz, cx_n, cz_n, ny, lan...]
where the time goes in v5:
time: 42 us; the launch traced here: 41.8 us
  Pallas kernels  39.9 us (95%)
  local copies, waits for them, and re-layouts  1.31 us (3%)
  between operations  0.64 us (2%)
    pallas_call x1, Pallas kernels, body(): pl.pallas_call(functools.partial(kernel, (n_gx, n_gz, cx_n, cz_n, ny, lan...  39.9 us
    unnamed x2, local copies, waits for them, and re-layouts  1.31 us

profile of v5, /device:TPU:0, one launch (start us, length us, event | category | flops | bytes accessed | tf_op | source)
XLA Modules:
  0.0 41.8 jit_solution(17654078878746855292)
XLA Ops:
  0.6 39.9 %corrector.1 = (f32[3,128,128]{2,1,0:T(8,128)S(1)}, f32[128,128]{1,0:T(8,128)S(1)}) custom-call(f32[3,128,128]{2,1,0:T(8,128)} %bitcast.9, f32[3,128,128]{2,1,0:T(8,128)} %bitcast.10, f32[128,128]{1,0:T(8,128)} %bitcast.12, f32[3,128,128]{2,1,0:T(8,128)} %bitcast.11, s32[2,8,16]{2,1,0:T(8,128)} %bc_in.1, s32[128,128]{1,0:T(8,128)} %bitcast.13, f32[64,64]{1,0:T(8,128)} %inv_in.1), custom_call_target="tpu_custom_call" | custom-call | tf_op jit(solution)/shard_map/corrector/pallas_call | solution.py:572
  40.5 0.7 %copy.11 = f32[3,8,16,128]{3,2,1,0:T(8,128)} copy(f32[3,8,16,128]{3,2,1,0:T(8,128)S(1)} %bitcast.7) | data formatting | bytes 393216
  41.2 0.6 %copy.12 = f32[8,16,128]{2,1,0:T(8,128)} copy(f32[8,16,128]{2,1,0:T(8,128)S(1)} %bitcast.8) | data formatting | bytes 131072
